TPU v7x, 256 devices: a whole 4x4x8 slice. The times are simulated.
256 devices in a mesh: seq: 32 (over z, y_lo, core), head: 8 (over y_hi, x).
Axes of the slice: x: 4, y: 4 (y_hi: 2, y_lo: 2; y = y_hi * 2 + y_lo), z: 8, core: 2. Of those that a mesh axis runs over, the one named last changes fastest.
Arguments:
- normed_layer_input: bfloat16 [8192, 8192], P('seq', 'head'), may hold values from -6 to 6
- query_projection_input: bfloat16 [8192, 8192], P('seq', 'head'), may hold values from -9 to 9, as said below
- key_projection_input: bfloat16 [8192, 1024], P('seq', 'head'), may hold values from -9 to 9, as said below
- value_projection_input: bfloat16 [8192, 1024], P('seq', 'head'), may hold values from -6 to 6
- output_gradient: bfloat16 [8192, 8192], P('seq', 'head'), may hold values from -12 to 12
- adapter_down_weight: bfloat16 [3, 8, 8192], P(None, None, 'head'), may hold values from -0.0007324219 to 0.0007324219
- adapter_up_query: bfloat16 [8, 8192], P(None, 'head'), may hold values from -0.0007324219 to 0.0007324219
- adapter_up_kv: bfloat16 [2, 8, 1024], P(None, None, 'head'), may hold values from -0.001953125 to 0.001953125
Outputs:
- query_projection_gradient: bfloat16 [8192, 8192], P('seq', 'head')
- key_projection_gradient: bfloat16 [8192, 1024], P('seq', 'head')
- value_projection_gradient: bfloat16 [8192, 1024], P('seq', 'head')
- adapter_down_gradient: float32 [3, 8, 8192], P(None, None, 'head')
- adapter_up_query_gradient: float32 [8, 8192], P(None, 'head')
- adapter_up_kv_gradient: float32 [2, 8, 1024], P(None, None, 'head')
Inputs may be any that keep to these rules, and one draw needn't show every extreme that they name: `query_projection_input`: real values. `key_projection_input`: real values.
All inputs are finite; a program needn't handle non-finite values.
Results may differ from a plain program's by a relative error of at most 0.029.
Values may be sent and summed in bfloat16 or wider, within the bound.
A program may use at most 64 MiB of HBM per device.

v0:
```python
import jax
import jax.numpy as jnp
from jax import lax
from jax.sharding import PartitionSpec as P

HEAD_SIZE = 128


position_scale = 0.04096


def from_behind(value, axis, steps):
    count = lax.axis_size(axis)
    pairs = [(source, (source + steps) % count) for source in range(count)]
    return lax.ppermute(value, axis, pairs)


def rope_tables(positions, feature_count):
    half_width = feature_count // 2
    frequency = position_scale * 10000.0 ** (
        -2.0 * jnp.arange(half_width, dtype=jnp.float32) / feature_count
    )
    angles = positions.astype(jnp.float32)[:, None] * frequency[None, :]
    return (jnp.cos(angles)[:, None, :], jnp.sin(angles)[:, None, :])


def rotate(vectors, cosine_table, sine_table):
    half_width = vectors.shape[-1] // 2
    low_half = vectors[..., :half_width]
    high_half = vectors[..., half_width:]
    return jnp.concatenate(
        [
            low_half * cosine_table - high_half * sine_table,
            high_half * cosine_table + low_half * sine_table,
        ],
        axis=-1,
    )


def unrotate(gradient, cosine_table, sine_table):
    half_width = gradient.shape[-1] // 2
    low_half = gradient[..., :half_width]
    high_half = gradient[..., half_width:]
    return jnp.concatenate(
        [
            low_half * cosine_table + high_half * sine_table,
            high_half * cosine_table - low_half * sine_table,
        ],
        axis=-1,
    )


def body(
    normed_layer_input,
    query_projection_input,
    key_projection_input,
    value_projection_input,
    output_gradient,
    adapter_down_weight,
    adapter_up_query,
    adapter_up_kv,
):
    tok_rows = query_projection_input.shape[0]
    query_count = query_projection_input.shape[1] // HEAD_SIZE
    query_width = query_count * HEAD_SIZE
    seq_count = lax.axis_size("seq")
    head_axis_count = lax.axis_size("head")
    group_dev = seq_count // 4
    half_offset = seq_count // 8
    seq_index = lax.axis_index("seq")
    shifted = lax.axis_index("head") >= head_axis_count // 2
    group_place = jnp.where(shifted, (seq_index - half_offset) % seq_count, seq_index) % group_dev
    positions = seq_index * tok_rows + jnp.arange(tok_rows, dtype=jnp.int32)
    cosine_table, sine_table = rope_tables(positions, HEAD_SIZE)
    query_rot = rotate(
        query_projection_input.astype(jnp.float32).reshape(tok_rows, query_count, HEAD_SIZE),
        cosine_table,
        sine_table,
    ).astype(jnp.bfloat16)
    key_rot = (
        rotate(
            key_projection_input.astype(jnp.float32).reshape(tok_rows, 1, HEAD_SIZE),
            cosine_table,
            sine_table,
        )
        .astype(jnp.bfloat16)
        .reshape(tok_rows, HEAD_SIZE)
    )
    grad_heads = output_gradient.reshape(tok_rows, query_count, HEAD_SIZE)
    key_value = jnp.concatenate([key_rot, value_projection_input], axis=1)
    block_list = [key_value]
    moving = key_value
    for cycle_step in range(group_dev - 1):
        moving = from_behind(moving, "seq", 1)
        block_list.append(moving)
    blocks = jnp.stack(block_list)
    key_all = blocks[:, :, :HEAD_SIZE].reshape(group_dev * tok_rows, HEAD_SIZE)
    value_all = blocks[:, :, HEAD_SIZE:].reshape(group_dev * tok_rows, HEAD_SIZE)
    score_scale = HEAD_SIZE ** (-0.5)
    query_pos = jnp.arange(tok_rows, dtype=jnp.int32)[:, None]
    column = jnp.arange(group_dev * tok_rows, dtype=jnp.int32)[None, :]
    source_block = column // tok_rows
    allowed = (group_place >= source_block) & (
        (source_block > 0) | (column % tok_rows <= query_pos)
    )
    heads_step = max(1, min(query_count, 512 // tok_rows))
    while query_count % heads_step != 0:
        heads_step = heads_step - 1
    step_count = query_count // heads_step
    query_steps = query_rot.reshape(tok_rows, step_count, heads_step, HEAD_SIZE).transpose(
        1, 0, 2, 3
    )
    grad_steps = grad_heads.reshape(tok_rows, step_count, heads_step, HEAD_SIZE).transpose(
        1, 0, 2, 3
    )

    def head_block(operands):
        query_blk, grad_blk = operands
        scores = (
            jnp.einsum("qhd,kd->hqk", query_blk, key_all, preferred_element_type=jnp.float32)
            * score_scale
        )
        masked = jnp.where(allowed, scores, -jnp.inf)
        row_top = jnp.max(masked, axis=-1, keepdims=True)
        log_total = row_top + jnp.log(jnp.sum(jnp.exp(masked - row_top), axis=-1, keepdims=True))
        weights = jnp.where(allowed, jnp.exp(scores - log_total), 0.0)
        prob_bf16 = weights.astype(jnp.bfloat16)
        attn_out = jnp.einsum(
            "hqk,kd->qhd", prob_bf16, value_all, preferred_element_type=jnp.float32
        ).astype(jnp.bfloat16)
        row_delta = jnp.sum(attn_out.astype(jnp.float32) * grad_blk.astype(jnp.float32), axis=-1).T[
            :, :, None
        ]
        prob_grad = jnp.einsum(
            "qhd,kd->hqk", grad_blk, value_all, preferred_element_type=jnp.float32
        )
        dscore = (weights * (prob_grad - row_delta)).astype(jnp.bfloat16)
        query_part = (
            jnp.einsum("hqk,kd->qhd", dscore, key_all, preferred_element_type=jnp.float32)
            * score_scale
        )
        key_part = (
            jnp.einsum("hqk,qhd->kd", dscore, query_blk, preferred_element_type=jnp.float32)
            * score_scale
        )
        value_part = jnp.einsum(
            "hqk,qhd->kd", prob_bf16, grad_blk, preferred_element_type=jnp.float32
        )
        return (query_part, key_part, value_part, log_total[:, :, 0], row_delta[:, :, 0])

    results = lax.map(head_block, (query_steps, grad_steps))
    query_rot_grad = results[0].transpose(1, 0, 2, 3).reshape(tok_rows, query_count, HEAD_SIZE)
    key_terms = jnp.sum(results[1], axis=0)
    value_terms = jnp.sum(results[2], axis=0)
    block_terms = jnp.stack(
        [
            key_terms.reshape(group_dev, tok_rows, HEAD_SIZE),
            value_terms.reshape(group_dev, tok_rows, HEAD_SIZE),
        ],
        axis=1,
    )
    carried = block_terms[group_dev - 1]
    for offset_back in range(group_dev - 2, -1, -1):
        carried = (
            from_behind(carried.astype(jnp.bfloat16), "seq", -1).astype(carried.dtype)
            + block_terms[offset_back]
        )
    query_gradient = (
        unrotate(query_rot_grad, cosine_table, sine_table)
        .astype(jnp.bfloat16)
        .reshape(tok_rows, query_width)
    )
    key_gradient = (
        unrotate(carried[0].reshape(tok_rows, 1, HEAD_SIZE), cosine_table, sine_table)
        .astype(jnp.bfloat16)
        .reshape(tok_rows, HEAD_SIZE)
    )
    value_gradient = carried[1].astype(jnp.bfloat16)
    kv_pile = jnp.stack([key_gradient, value_gradient])
    down_piece = jnp.einsum(
        "zg,wfg->zwf", normed_layer_input, adapter_down_weight, preferred_element_type=jnp.float32
    )
    back_query = jnp.dot(query_gradient, adapter_up_query.T, preferred_element_type=jnp.float32)
    back_pair = jnp.einsum(
        "xfn,xqn->fxq", kv_pile, adapter_up_kv, preferred_element_type=jnp.float32
    )
    backward_piece = jnp.concatenate([back_query[:, None, :], back_pair], axis=1)
    down_sum, back_sum = (
        lax.psum(down_piece.astype(jnp.bfloat16), "head").astype(jnp.float32),
        lax.psum(backward_piece.astype(jnp.bfloat16), "head").astype(jnp.float32),
    )
    down_activation = down_sum.astype(jnp.bfloat16)
    backward_activation = back_sum.astype(jnp.bfloat16)
    up_query_local = 2.0 * jnp.einsum(
        "yj,yq->jq", down_activation[:, 0], query_gradient, preferred_element_type=jnp.float32
    )
    up_pair_local = 2.0 * jnp.einsum(
        "yij,iyq->ijq", down_activation[:, 1:], kv_pile, preferred_element_type=jnp.float32
    )
    down_local = 2.0 * jnp.einsum(
        "yhu,ym->hum", backward_activation, normed_layer_input, preferred_element_type=jnp.float32
    )
    down_total, up_query_total, up_pair_total = (
        lax.psum(down_local.astype(jnp.bfloat16), "seq").astype(jnp.float32),
        lax.psum(up_query_local.astype(jnp.bfloat16), "seq").astype(jnp.float32),
        lax.psum(up_pair_local.astype(jnp.bfloat16), "seq").astype(jnp.float32),
    )
    return (query_gradient, key_gradient, value_gradient, down_total, up_query_total, up_pair_total)


def solution(mesh):
    placed = (
        P("seq", "head"),
        P("seq", "head"),
        P("seq", "head"),
        P("seq", "head"),
        P("seq", "head"),
        P(None, None, "head"),
        P(None, "head"),
        P(None, None, "head"),
    )
    return jax.shard_map(
        body,
        mesh=mesh,
        in_specs=placed,
        out_specs=(
            P("seq", "head"),
            P("seq", "head"),
            P("seq", "head"),
            P(None, None, "head"),
            P(None, "head"),
            P(None, None, "head"),
        ),
        check_vma=False,
    )
```

profile of v0, /device:TPU:1, one launch (start us, length us, event | category | flops | bytes accessed | tf_op | source)
XLA Modules:
  0.0 416.1 jit_solution(2638873507155498322)
XLA Ops:
  8.8 1.6 bitcast_dynamic-update-slice_fusion.7
  10.4 2.7 collective-permute-start
  15.0 1.3 subtract_convert_fusion
  17.6 2.0 copy.29
  20.0 1.6 bitcast_dynamic-update-slice_fusion.6
  22.2 2.3 collective-permute-start.2
  25.2 3.6 collective-permute-done.2
  29.6 5.7 %collective-permute-done.3 = bf16[256,256]{1,0:T(8,128)(2,1)S(1)} collective-permute-done((bf16[256,256]{1,0:T(8,128)(2,1)S(1)}, bf16[256,256]{1,0:T(8,128)(2,1)S(1)}, u32[]{:S(2)}, u32[]{:S(2)}) %collective-permute-start.3) | collective-permute-done | bytes 131104 | tf_op jit(solution)/shard_map/ppermute | solution.py:15
  36.0 5.8 %collective-permute-done.4 = bf16[256,256]{1,0:T(8,128)(2,1)S(1)} collective-permute-done((bf16[256,256]{1,0:T(8,128)(2,1)S(1)}, bf16[256,256]{1,0:T(8,128)(2,1)S(1)}, u32[]{:S(2)}, u32[]{:S(2)}) %collective-permute-start.4) | collective-permute-done | bytes 131104 | tf_op jit(solution)/shard_map/ppermute | solution.py:15
  42.5 5.8 %collective-permute-done.5 = bf16[256,256]{1,0:T(8,128)(2,1)S(1)} collective-permute-done((bf16[256,256]{1,0:T(8,128)(2,1)S(1)}, bf16[256,256]{1,0:T(8,128)(2,1)S(1)}, u32[]{:S(2)}, u32[]{:S(2)}) %collective-permute-start.5) | collective-permute-done | bytes 131104 | tf_op jit(solution)/shard_map/ppermute | solution.py:15
  49.0 5.8 %collective-permute-done.6 = bf16[256,256]{1,0:T(8,128)(2,1)S(1)} collective-permute-done((bf16[256,256]{1,0:T(8,128)(2,1)S(1)}, bf16[256,256]{1,0:T(8,128)(2,1)S(1)}, u32[]{:S(2)}, u32[]{:S(2)}) %collective-permute-start.6) | collective-permute-done | bytes 131104 | tf_op jit(solution)/shard_map/ppermute | solution.py:15
  55.5 1.3 fusion.101
  57.8 56.7 %while.15 = (s32[]{:T(128)}, f32[4,256,2,128]{3,1,2,0:T(8,128)S(1)}, f32[4,2048,128]{2,1,0:T(8,128)}, f32[4,2048,128]{2,1,0:T(8,128)}, bf16[4,256,2,128]{3,1,2,0...) while((s32[]{:T(128)}, ...), condition=%wide.region_4.5_spmd.clone, body=%wide.region_0.4_spmd.clone.sunk | while | flops 1634860032 | bytes 71749384 | solution.py:151
  59.3 1.2 exponential_reduce_fusion.2
  61.7 2.3 fusion.144
  64.2 3.7 fusion.140
  67.9 1.7 fusion.141
  69.5 1.8 fusion.143
  73.5 1.2 exponential_reduce_fusion.2
  75.9 2.3 fusion.144
  78.3 3.7 fusion.140
  82.1 1.7 fusion.141
  83.7 1.7 fusion.143
  87.7 1.2 exponential_reduce_fusion.2
  90.0 2.3 fusion.144
  92.4 3.7 fusion.140
  96.2 1.6 fusion.141
  97.8 1.7 fusion.143
  104.1 2.4 fusion.144
  106.7 3.7 fusion.140
  110.4 1.6 fusion.141
  112.1 1.7 fusion.143
  114.5 2.8 reduce_sum.36
  117.4 2.5 reduce_sum.37
  119.9 5.7 %collective-permute-start.7 = (bf16[2,256,128]{2,1,0:T(8,128)(2,1)S(1)}, bf16[2,256,128]{2,1,0:T(8,128)(2,1)S(1)}, u32[]{:S(2)}, u32[]{:S(2)}) collective-permute-start(bf16[2,256,128]{2,1,0:T(8,128)(2,1)S(1)} %fusion.86), channel_id=1, source_target_pairs={{0,248},{8,0},{16,8},{24,16},{32,24},{40,32},{48,40},{56,48},{64,5... | collective-permute-start | bytes 393224 | tf_op jit(solution)/shard_map/ppermute | solution.py:15
  126.7 1.6 collective-permute-start.8
  128.3 2.9 collective-permute-done.8
  131.2 3.7 collective-permute-start.9
  136.0 5.8 %collective-permute-start.10 = (bf16[2,256,128]{2,1,0:T(8,128)(2,1)S(1)}, bf16[2,256,128]{2,1,0:T(8,128)(2,1)S(1)}, u32[]{:S(2)}, u32[]{:S(2)}) collective-permute-start(bf16[2,256,128]{2,1,0:T(8,128)(2,1)S(1)} %fusion.59), channel_id=1, source_target_pairs={{0,248},{8,0},{16,8},{24,16},{32,24},{40,32},{48,40},{56,48},{64,5... | collective-permute-start | bytes 393224 | tf_op jit(solution)/shard_map/ppermute | solution.py:15
  142.8 5.6 %collective-permute-start.11 = (bf16[2,256,128]{2,1,0:T(8,128)(2,1)S(1)}, bf16[2,256,128]{2,1,0:T(8,128)(2,1)S(1)}, u32[]{:S(2)}, u32[]{:S(2)}) collective-permute-start(bf16[2,256,128]{2,1,0:T(8,128)(2,1)S(1)} %fusion.63), channel_id=1, source_target_pairs={{0,248},{8,0},{16,8},{24,16},{32,24},{40,32},{48,40},{56,48},{64,5... | collective-permute-start | bytes 393224 | tf_op jit(solution)/shard_map/ppermute | solution.py:15
  149.4 5.6 %collective-permute-start.12 = (bf16[2,256,128]{2,1,0:T(8,128)(2,1)S(1)}, bf16[2,256,128]{2,1,0:T(8,128)(2,1)S(1)}, u32[]{:S(2)}, u32[]{:S(2)}) collective-permute-start(bf16[2,256,128]{2,1,0:T(8,128)(2,1)S(1)} %fusion.67), channel_id=1, source_target_pairs={{0,248},{8,0},{16,8},{24,16},{32,24},{40,32},{48,40},{56,48},{64,5... | collective-permute-start | bytes 393224 | tf_op jit(solution)/shard_map/ppermute | solution.py:15
  155.0 1.4 multiply_add_fusion
  156.9 4.8 %collective-permute-start.13 = (bf16[2,256,128]{2,1,0:T(8,128)(2,1)S(1)}, bf16[2,256,128]{2,1,0:T(8,128)(2,1)S(1)}, u32[]{:S(2)}, u32[]{:S(2)}) collective-permute-start(bf16[2,256,128]{2,1,0:T(8,128)(2,1)S(1)} %fusion.45), channel_id=1, source_target_pairs={{0,248},{8,0},{16,8},{24,16},{32,24},{40,32},{48,40},{56,48},{64,5... | collective-permute-start | bytes 393224 | tf_op jit(solution)/shard_map/ppermute | solution.py:15
  163.5 34.5 %all-reduce.1 = (bf16[256,3,8]{0,2,1:T(8,128)(2,1)S(1)}, bf16[256,3,8]{0,2,1:T(8,128)(2,1)S(1)}) all-reduce(bf16[256,3,8]{0,2,1:T(8,128)(2,1)S(1)} %pad_maximum_fusion.6, bf16[256,3,8]{0,2,1:T(8,128)(2,1)S(1)} %convolution_convert_fusion.1), channel_id=1, replica_groups=mesh['seq'=32,'head'=8] {'head'}, use_global_device_ids=true, to_apply=%region_7.8 | all-reduce | flops 12288 | bytes 49152 | tf_op jit(solution)/shard_map/psum | solution.py:190
  201.8 203.4 %all-reduce.4.cloned.1.call-done = (bf16[3,8,1024]{2,1,0:T(8,128)(2,1)}, bf16[8,1024]{1,0:T(8,128)(2,1)}, bf16[2,8,128]{2,1,0:T(8,128)(2,1)}) async-done(((bf16[3,8,1024]{2,1,0:T(8,128)(2,1)}, bf16[8,1024]{1,0:T(8,128)(2,1)}, bf16[2,8,128]{2,1,0:T(8,128)(2,1)}), (bf16[3,8,1024]{2,1,0:T(8,128)(2,1)}, bf16[8,1024]{1,0:T(8,128)(2,1)}, bf16[2,8,128]{2,1,0:T(8,128)(2,1)})) %all-reduce.4.cloned.1.call-update) | async-done | bytes 69648 | tf_op jit(solution)/shard_map/psum | solution.py:204
  405.2 1.4 convert_element_type.155
  406.7 1.3 convert_element_type.158
  408.0 1.3 convert_element_type.160
  (151 shorter events, 36.0 us)
Async XLA Ops:
  7.2 134.6 %copy-start = (bf16[256,1024]{1,0:T(8,128)(2,1)S(1)}, bf16[256,1024]{1,0:T(8,128)(2,1)}, u32[]{:S(2)}) copy-start(bf16[256,1024]{1,0:T(8,128)(2,1)} %param.10) | copy-start | bytes 1572868
  7.2 398.0 %all-reduce.4.cloned.1.call-start = ((), (), s32[]{:S(2)}) async-start(), calls=%async_computation | async-start | bytes 139264 | tf_op jit(solution)/shard_map/psum | solution.py:204
  7.2 9.1 %copy-start.15 = (f32[64]{0:T(128)}, f32[64]{0:T(128)S(1)}, u32[]{:S(2)}) copy-start(f32[64]{0:T(128)S(1)} %power_multiply_fusion) | copy-start | bytes 772
  7.3 9.0 %copy-start.13 = (f32[256]{0:T(256)}, f32[256]{0:T(256)S(1)}, u32[]{:S(2)}) copy-start(f32[256]{0:T(256)S(1)} %add_convert_fusion.1) | copy-start | bytes 3076
  10.4 9.5 %collective-permute-start = (bf16[256,256]{1,0:T(8,128)(2,1)S(1)}, bf16[256,256]{1,0:T(8,128)(2,1)}, u32[]{:S(2)}, u32[]{:S(2)}) collective-permute-start(bf16[256,256]{1,0:T(8,128)(2,1)S(1)} %get-tuple-element.124), channel_id=1, source_target_pairs={{0,8},{8,16},{16,24},{24,32},{32,40},{40,48},{48,56},{56,64},{64,7... | collective-permute-start | bytes 393224 | tf_op jit(solution)/shard_map/ppermute | solution.py:15
  13.6 3.9 copy-start.6
  19.9 2.3 collective-permute-start.1
  22.2 6.6 %collective-permute-start.2 = (bf16[256,256]{1,0:T(8,128)(2,1)S(1)}, bf16[256,256]{1,0:T(8,128)(2,1)S(1)}, u32[]{:S(2)}, u32[]{:S(2)}) collective-permute-start(bf16[256,256]{1,0:T(8,128)(2,1)S(1)} %collective-permute-done.1), channel_id=1, source_target_pairs={{0,8},{8,16},{16,24},{24,32},{32,40},{40,48},{48,56},{56,64},{64,7... | collective-permute-start | bytes 393224 | tf_op jit(solution)/shard_map/ppermute | solution.py:15
  28.8 6.5 %collective-permute-start.3 = (bf16[256,256]{1,0:T(8,128)(2,1)S(1)}, bf16[256,256]{1,0:T(8,128)(2,1)S(1)}, u32[]{:S(2)}, u32[]{:S(2)}) collective-permute-start(bf16[256,256]{1,0:T(8,128)(2,1)S(1)} %collective-permute-done.2), channel_id=1, source_target_pairs={{0,8},{8,16},{16,24},{24,32},{32,40},{40,48},{48,56},{56,64},{64,7... | collective-permute-start | bytes 393224 | tf_op jit(solution)/shard_map/ppermute | solution.py:15
  35.3 6.5 %collective-permute-start.4 = (bf16[256,256]{1,0:T(8,128)(2,1)S(1)}, bf16[256,256]{1,0:T(8,128)(2,1)S(1)}, u32[]{:S(2)}, u32[]{:S(2)}) collective-permute-start(bf16[256,256]{1,0:T(8,128)(2,1)S(1)} %collective-permute-done.3), channel_id=1, source_target_pairs={{0,8},{8,16},{16,24},{24,32},{32,40},{40,48},{48,56},{56,64},{64,7... | collective-permute-start | bytes 393224 | tf_op jit(solution)/shard_map/ppermute | solution.py:15
  41.8 6.5 %collective-permute-start.5 = (bf16[256,256]{1,0:T(8,128)(2,1)S(1)}, bf16[256,256]{1,0:T(8,128)(2,1)S(1)}, u32[]{:S(2)}, u32[]{:S(2)}) collective-permute-start(bf16[256,256]{1,0:T(8,128)(2,1)S(1)} %collective-permute-done.4), channel_id=1, source_target_pairs={{0,8},{8,16},{16,24},{24,32},{32,40},{40,48},{48,56},{56,64},{64,7... | collective-permute-start | bytes 393224 | tf_op jit(solution)/shard_map/ppermute | solution.py:15
  48.3 6.5 %collective-permute-start.6 = (bf16[256,256]{1,0:T(8,128)(2,1)S(1)}, bf16[256,256]{1,0:T(8,128)(2,1)S(1)}, u32[]{:S(2)}, u32[]{:S(2)}) collective-permute-start(bf16[256,256]{1,0:T(8,128)(2,1)S(1)} %collective-permute-done.5), channel_id=1, source_target_pairs={{0,8},{8,16},{16,24},{24,32},{32,40},{40,48},{48,56},{56,64},{64,7... | collective-permute-start | bytes 393224 | tf_op jit(solution)/shard_map/ppermute | solution.py:15
  59.3 2.3 copy-start.1
  60.5 1.1 copy-start.9
  64.1 3.7 copy-start.2
  64.1 3.7 copy-start.8
  64.1 3.7 copy-start.10
  73.5 2.3 copy-start.1
  74.8 1.1 copy-start.9
  78.3 3.7 copy-start.2
  78.3 3.7 copy-start.8
  78.3 3.7 copy-start.10
  87.6 2.3 copy-start.1
  88.9 1.1 copy-start.9
  92.4 3.7 copy-start.2
  92.4 3.7 copy-start.8
  92.4 3.7 copy-start.10
  101.8 2.3 copy-start.1
  103.0 1.1 copy-start.9
  106.7 3.7 copy-start.2
  106.7 3.7 copy-start.8
  106.7 3.7 copy-start.10
  114.5 2.9 copy-start.4
  119.9 21.9 %copy-start.11 = (bf16[3,8,1024]{2,1,0:T(8,128)(2,1)S(1)}, bf16[3,8,1024]{2,1,0:T(8,128)(2,1)}, u32[]{:S(2)}) copy-start(bf16[3,8,1024]{2,1,0:T(8,128)(2,1)} %param.15) | copy-start | bytes 147460
  119.9 6.7 %collective-permute-start.7 = (bf16[2,256,128]{2,1,0:T(8,128)(2,1)S(1)}, bf16[2,256,128]{2,1,0:T(8,128)(2,1)S(1)}, u32[]{:S(2)}, u32[]{:S(2)}) collective-permute-start(bf16[2,256,128]{2,1,0:T(8,128)(2,1)S(1)} %fusion.86), channel_id=1, source_target_pairs={{0,248},{8,0},{16,8},{24,16},{32,24},{40,32},{48,40},{56,48},{64,5... | collective-permute-start | bytes 393224 | tf_op jit(solution)/shard_map/ppermute | solution.py:15
  126.7 21.7 %copy-start.5 = (f32[4,256,2,128]{3,1,2,0:T(8,128)S(1)}, f32[4,256,2,128]{3,1,2,0:T(8,128)}, u32[]{:S(2)}) copy-start(f32[4,256,2,128]{3,1,2,0:T(8,128)} %copy-done.4) | copy-start | bytes 3145732
  126.7 4.5 %collective-permute-start.8 = (bf16[2,256,128]{2,1,0:T(8,128)(2,1)S(1)}, bf16[2,256,128]{2,1,0:T(8,128)(2,1)S(1)}, u32[]{:S(2)}, u32[]{:S(2)}) collective-permute-start(bf16[2,256,128]{2,1,0:T(8,128)(2,1)S(1)} %fusion.51), channel_id=1, source_target_pairs={{0,248},{8,0},{16,8},{24,16},{32,24},{40,32},{48,40},{56,48},{64,5... | collective-permute-start | bytes 393224 | tf_op jit(solution)/shard_map/ppermute | solution.py:15
  131.2 4.7 %collective-permute-start.9 = (bf16[2,256,128]{2,1,0:T(8,128)(2,1)S(1)}, bf16[2,256,128]{2,1,0:T(8,128)(2,1)S(1)}, u32[]{:S(2)}, u32[]{:S(2)}) collective-permute-start(bf16[2,256,128]{2,1,0:T(8,128)(2,1)S(1)} %fusion.55), channel_id=1, source_target_pairs={{0,248},{8,0},{16,8},{24,16},{32,24},{40,32},{48,40},{56,48},{64,5... | collective-permute-start | bytes 393224 | tf_op jit(solution)/shard_map/ppermute | solution.py:15
  136.0 6.8 %collective-permute-start.10 = (bf16[2,256,128]{2,1,0:T(8,128)(2,1)S(1)}, bf16[2,256,128]{2,1,0:T(8,128)(2,1)S(1)}, u32[]{:S(2)}, u32[]{:S(2)}) collective-permute-start(bf16[2,256,128]{2,1,0:T(8,128)(2,1)S(1)} %fusion.59), channel_id=1, source_target_pairs={{0,248},{8,0},{16,8},{24,16},{32,24},{40,32},{48,40},{56,48},{64,5... | collective-permute-start | bytes 393224 | tf_op jit(solution)/shard_map/ppermute | solution.py:15
  142.0 13.0 %copy-start.7 = (f32[256,64]{1,0:T(8,128)S(1)}, f32[256,64]{1,0:T(8,128)}, u32[]{:S(2)}) copy-start(f32[256,64]{1,0:T(8,128)} %copy-done.6) | copy-start | bytes 196612
  142.8 6.6 %collective-permute-start.11 = (bf16[2,256,128]{2,1,0:T(8,128)(2,1)S(1)}, bf16[2,256,128]{2,1,0:T(8,128)(2,1)S(1)}, u32[]{:S(2)}, u32[]{:S(2)}) collective-permute-start(bf16[2,256,128]{2,1,0:T(8,128)(2,1)S(1)} %fusion.63), channel_id=1, source_target_pairs={{0,248},{8,0},{16,8},{24,16},{32,24},{40,32},{48,40},{56,48},{64,5... | collective-permute-start | bytes 393224 | tf_op jit(solution)/shard_map/ppermute | solution.py:15
  149.4 7.4 %collective-permute-start.12 = (bf16[2,256,128]{2,1,0:T(8,128)(2,1)S(1)}, bf16[2,256,128]{2,1,0:T(8,128)(2,1)S(1)}, u32[]{:S(2)}, u32[]{:S(2)}) collective-permute-start(bf16[2,256,128]{2,1,0:T(8,128)(2,1)S(1)} %fusion.67), channel_id=1, source_target_pairs={{0,248},{8,0},{16,8},{24,16},{32,24},{40,32},{48,40},{56,48},{64,5... | collective-permute-start | bytes 393224 | tf_op jit(solution)/shard_map/ppermute | solution.py:15
  155.0 6.6 %copy-start.12 = (bf16[8,1024]{1,0:T(8,128)(2,1)S(1)}, bf16[8,1024]{1,0:T(8,128)(2,1)}, u32[]{:S(2)}) copy-start(bf16[8,1024]{1,0:T(8,128)(2,1)} %param.16) | copy-start | bytes 49156
  156.4 6.3 %copy-start.14 = (f32[256]{0:T(256)S(1)}, f32[256]{0:T(256)}, u32[]{:S(2)}) copy-start(f32[256]{0:T(256)} %copy-done.13) | copy-start | bytes 3076
  156.4 6.3 %copy-start.16 = (f32[64]{0:T(128)S(1)}, f32[64]{0:T(128)}, u32[]{:S(2)}) copy-start(f32[64]{0:T(128)} %copy-done.15) | copy-start | bytes 772
  156.4 6.9 %copy-start.17 = (bf16[2,8,128]{2,1,0:T(8,128)(2,1)S(1)}, bf16[2,8,128]{2,1,0:T(8,128)(2,1)}, u32[]{:S(2)}) copy-start(bf16[2,8,128]{2,1,0:T(8,128)(2,1)} %param.17) | copy-start | bytes 12292
  156.8 45.0 %copy-start.3 = (bf16[32,8,8,128]{3,1,2,0:T(8,128)(2,1)}, bf16[32,8,8,128]{3,1,2,0:T(8,128)(2,1)S(1)}, u32[]{:S(2)}) copy-start(bf16[32,8,8,128]{3,1,2,0:T(8,128)(2,1)S(1)} %copy.50) | copy-start | bytes 1572868
  156.9 5.7 %collective-permute-start.13 = (bf16[2,256,128]{2,1,0:T(8,128)(2,1)S(1)}, bf16[2,256,128]{2,1,0:T(8,128)(2,1)S(1)}, u32[]{:S(2)}, u32[]{:S(2)}) collective-permute-start(bf16[2,256,128]{2,1,0:T(8,128)(2,1)S(1)} %fusion.45), channel_id=1, source_target_pairs={{0,248},{8,0},{16,8},{24,16},{32,24},{40,32},{48,40},{56,48},{64,5... | collective-permute-start | bytes 393224 | tf_op jit(solution)/shard_map/ppermute | solution.py:15
Sparse Core Ops, SparseCore 0:
  201.2 203.9 all-reduce.3
where the time goes:
time: 417 us; the launch traced here: 416 us
  waiting for transfers between devices  238 us (57%)
  matrix products  47.8 us (11%)
  starting transfers between devices  38.1 us (9%)
  blocking collectives  34.5 us (8%)
  other arithmetic  25.6 us (6%)
  local copies, waits for them, and re-layouts  17.4 us (4%)
  between operations  14.4 us (3%)
    psum x1, waiting for transfers between devices, body(): lax.psum(down_local.astype(jnp.bfloat16), 'seq').astype(jnp.float32)  203 us
    ppermute x14, starting transfers between devices, from_behind(): return lax.ppermute(value, axis, pairs)  38.1 us
    psum x1, blocking collectives, body(): lax.psum(backward_piece.astype(jnp.bfloat16), 'head').astype(jnp.float32)  34.5 us
    ppermute x14, waiting for transfers between devices, from_behind(): return lax.ppermute(value, axis, pairs)  34.3 us
    dot_general x4, matrix products, head_block(): jnp.einsum('hqk,kd->qhd', prob_bf16, value_all, preferred_element_type=jn...  14.7 us
    dot_general x4, matrix products, head_block(): jnp.einsum('hqk,qhd->kd', prob_bf16, grad_blk, preferred_element_type=jnp...  9.35 us
  transfers between devices with their start and end apart: 15, of which 13 were waited for; matrix products, arithmetic and copies ran while one was open for 4% of the time, Pallas kernels for 0%

commit v1 on v0

v1 whole, which is shorter than its diff:
```python
import functools

import jax
import jax.numpy as jnp
from jax import lax
from jax.experimental import pallas as pl
from jax.experimental.pallas import tpu as pltpu
from jax.sharding import PartitionSpec as P

HEAD_SIZE = 128
POSITION_SCALE = 0.04096
LOG2E = 1.4426950408889634
MESH = pl.DeviceIdType.MESH
F32 = jnp.float32
BF16 = jnp.bfloat16
GROUP = 8
QUAD = 4
NT = (((1,), (1,)), ((), ()))


def dot(a, b):
    return jnp.dot(a, b, preferred_element_type=F32)


def dot_nt(a, b):
    return lax.dot_general(a, b, NT, preferred_element_type=F32)


def kernel(
    seq_count,
    head_count,
    q_ref,
    k_ref,
    v_ref,
    do_ref,
    x_ref,
    wd_ref,
    uq_ref,
    ukv_ref,
    dq_ref,
    dk_ref,
    dv_ref,
    gd_ref,
    guq_ref,
    gukv_ref,
    kv_all,
    kt_all,
    q_rot,
    do_hm,
    e_buf,
    dp_buf,
    m_blk,
    m_run,
    l_run,
    d_run,
    p_t,
    ds_t,
    dq_t,
    acc,
    part_out,
    pair_in,
    chip_in,
    down_out,
    down_in,
    back_out,
    back_in,
    rs1_out,
    rs1_in,
    z1_out,
    z1_in,
    g1_out,
    g1_in,
    rs2_out,
    rs2_in,
    z2_out,
    z2_in,
    g2_out,
    g2_in,
    kv_s,
    kv_r,
    fw_s,
    part_s,
    pair_r,
    chip_r,
    down_s,
    down_r,
    back_s,
    back_r,
    rs1_s,
    rs1_r,
    z1_s,
    z1_r,
    g1_s,
    g1_r,
    rs2_s,
    rs2_r,
    z2_s,
    z2_r,
    g2_s,
    g2_r,
):
    rows = k_ref.shape[0]
    heads = q_ref.shape[1] // HEAD_SIZE
    width = heads * HEAD_SIZE
    score_scale = HEAD_SIZE ** -0.5
    s = lax.axis_index("seq")
    h = lax.axis_index("head")
    shift = jnp.where(h >= head_count // 2, GROUP // 2, 0)
    place = (s + seq_count - shift) % GROUP
    chip = place // 2
    core = place % 2
    unit = s % QUAD
    z = s // QUAD
    z_count = seq_count // QUAD

    def at_place(q):
        return ((s + seq_count - place + q) % seq_count, h)

    partner = at_place(place + 1 - 2 * core)

    def at_head(i):
        return (s, i)

    def at_unit(i):
        return (z * QUAD + i, h)

    def at_z(i):
        return (i * QUAD + unit, h)

    def rc(src, dst, ss, rs, dev):
        return pltpu.make_async_remote_copy(
            src_ref=src, dst_ref=dst, send_sem=ss, recv_sem=rs, device_id=dev, device_id_type=MESH
        )

    barrier = pltpu.get_barrier_semaphore()

    def greet(i, carry):
        pl.semaphore_signal(barrier, inc=1, device_id=at_place((place + i) % GROUP), device_id_type=MESH)
        pl.semaphore_signal(barrier, inc=1, device_id=at_head((h + i) % head_count), device_id_type=MESH)
        pl.semaphore_signal(barrier, inc=1, device_id=at_z((z + i) % z_count), device_id_type=MESH)
        return carry

    lax.fori_loop(1, 8, greet, 0)

    half = HEAD_SIZE // 2
    lane = lax.broadcasted_iota(jnp.int32, (1, HEAD_SIZE), 1)
    feature = (lane % half).astype(F32)
    frequency = POSITION_SCALE * jnp.exp(feature * (-2.0 / HEAD_SIZE * 9.210340371976184))
    position = (s * rows + lax.broadcasted_iota(jnp.int32, (rows, 1), 0)).astype(F32)
    angle = position * frequency
    cosine = jnp.cos(angle)
    sine = jnp.where(lane < half, -1.0, 1.0) * jnp.sin(angle)

    def rotate(x):
        return x * cosine + pltpu.roll(x, half, 1) * sine

    def unrotate(x):
        return x * cosine - pltpu.roll(x, half, 1) * sine

    kv_all[place, 0] = rotate(k_ref[...].astype(F32)).astype(BF16)
    kv_all[place, 1] = v_ref[...]
    down_out[...] = dot_nt(wd_ref[...], x_ref[...]).astype(BF16)
    down_in[h] = down_out[...]
    for i in range(heads):
        cols = slice(i * HEAD_SIZE, (i + 1) * HEAD_SIZE)
        q_rot[i * rows : (i + 1) * rows, :] = rotate(q_ref[:, cols].astype(F32)).astype(BF16)
        do_hm[i * rows : (i + 1) * rows, :] = do_ref[:, cols]

    pl.semaphore_wait(barrier, 21)

    def kv_copy(q):
        return rc(kv_all.at[place], kv_all.at[place], kv_s.at[q], kv_r.at[place], at_place(q))

    @pl.when(core == 0)
    def _():
        kv_copy(place + 1).start()

    def kv_start(i, carry):
        kv_copy(2 * i + core).start()
        return carry

    lax.fori_loop(chip + 1, QUAD, kv_start, 0)

    def head_loop(fn):
        lax.fori_loop(1, head_count, lambda i, c: (fn((h + i) % head_count), c)[1], 0)

    head_loop(lambda i: rc(down_out, down_in.at[h], down_s.at[i], down_r.at[h], at_head(i)).start())

    def forward_block(j, masked):
        keys = kv_all[j, 0]
        values = kv_all[j, 1]
        kt_all[j] = keys.T
        for i in range(heads):
            span = slice(i * rows, (i + 1) * rows)
            st = dot_nt(keys, q_rot[span, :])
            dp = dot_nt(values, do_hm[span, :])
            if masked:
                key_pos = lax.broadcasted_iota(jnp.int32, (rows, rows), 0)
                query_pos = lax.broadcasted_iota(jnp.int32, (rows, rows), 1)
                st = jnp.where(key_pos <= query_pos, st, -1e30)
                top = jnp.max(st, axis=0, keepdims=True)
                e = jnp.exp2((st - top) * (score_scale * LOG2E))
                l_run[i] = jnp.sum(e, axis=0, keepdims=True)
                d_run[i] = jnp.sum(e * dp, axis=0, keepdims=True)
            else:
                old = m_run[i]
                top = jnp.maximum(old, jnp.max(st, axis=0, keepdims=True))
                e = jnp.exp2((st - top) * (score_scale * LOG2E))
                fix = jnp.exp2((old - top) * (score_scale * LOG2E))
                l_run[i] = l_run[i] * fix + jnp.sum(e, axis=0, keepdims=True)
                d_run[i] = d_run[i] * fix + jnp.sum(e * dp, axis=0, keepdims=True)
            m_run[i] = top
            m_blk[j, i] = top
            e_buf[j, :, span] = e
            dp_buf[j, :, span] = dp

    forward_block(place, True)

    def forward_step(u, carry):
        par = u % 2
        j = 2 * (chip - u // 2) + core + par * (1 - 2 * core)
        rc(kv_all.at[j], kv_all.at[j], kv_s.at[j], kv_r.at[j], partner).wait_recv()

        @pl.when(par == 0)
        def _():
            rc(kv_all.at[j], kv_all.at[j], fw_s.at[j], kv_r.at[j], partner).start()

        forward_block(j, False)
        return carry

    lax.fori_loop(2 - core, 2 * chip + 2, forward_step, 0)

    for i in range(heads):
        inv = 1.0 / l_run[i]
        l_run[i] = inv
        d_run[i] = d_run[i] * inv

    dq_t[...] = jnp.zeros_like(dq_t)

    def backward_block(j):
        for i in range(heads):
            span = slice(i * rows, (i + 1) * rows)
            scale = jnp.exp2((m_blk[j, i] - m_run[i]) * (score_scale * LOG2E)) * l_run[i]
            prob = e_buf[j, :, span] * scale
            p_t[:, span] = prob.astype(BF16)
            ds_t[:, span] = (prob * (dp_buf[j, :, span] - d_run[i])).astype(BF16)
        dq_t[...] += dot(kt_all[j], ds_t[...])
        return dot(ds_t[...], q_rot[...]), dot(p_t[...], do_hm[...])

    def part_copy_pair(j):
        return rc(part_out.at[j], pair_in.at[j], part_s.at[j], pair_r.at[j], partner)

    def part_copy_chip(j):
        return rc(part_out.at[j], chip_in.at[chip], part_s.at[j], chip_r.at[chip], at_place(j))

    def backward_step(w, carry):
        par = w % 2
        j = 2 * (w // 2) + (1 - core) + par * (2 * core - 1)
        key_part, value_part = backward_block(j)

        @pl.when(par == 0)
        def _():
            part_out[j, 0] = key_part.astype(BF16)
            part_out[j, 1] = value_part.astype(BF16)
            part_copy_pair(j).start()

        @pl.when(par == 1)
        def _():
            part_copy_pair(j).wait_recv()
            part_out[j, 0] = (key_part + pair_in[j, 0].astype(F32)).astype(BF16)
            part_out[j, 1] = (value_part + pair_in[j, 1].astype(F32)).astype(BF16)
            part_copy_chip(j).start()

        return carry

    lax.fori_loop(0, place, backward_step, 0)
    key_part, value_part = backward_block(place)
    acc[0] = key_part
    acc[1] = value_part

    back = jnp.zeros((8, rows), F32)
    for i in range(heads):
        span = slice(i * rows, (i + 1) * rows)
        cols = slice(i * HEAD_SIZE, (i + 1) * HEAD_SIZE)
        grad = unrotate(dq_t[:, span].T * score_scale).astype(BF16)
        dq_ref[:, cols] = grad
        back += dot_nt(uq_ref[:, cols], grad)
    back_out[0:8, :] = back.astype(BF16)

    @pl.when(core == 0)
    def _():
        rc(part_out.at[place], pair_in.at[place], part_s.at[place], pair_r.at[place], partner).wait_recv()
        acc[...] += pair_in[place].astype(F32)

    def chip_add(i, carry):
        rc(part_out.at[place], chip_in.at[i], part_s.at[place], chip_r.at[i], at_place(2 * i + core)).wait_recv()
        acc[...] += chip_in[i].astype(F32)
        return carry

    lax.fori_loop(chip + 1, QUAD, chip_add, 0)
    key_grad = unrotate(acc[0] * score_scale).astype(BF16)
    value_grad = acc[1].astype(BF16)
    dk_ref[...] = key_grad
    dv_ref[...] = value_grad
    back_out[8:16, :] = dot_nt(ukv_ref[0:8, :], key_grad).astype(BF16)
    back_out[16:24, :] = dot_nt(ukv_ref[8:16, :], value_grad).astype(BF16)
    back_in[h] = back_out[...]
    head_loop(lambda i: rc(back_out, back_in.at[h], back_s.at[i], back_r.at[h], at_head(i)).start())

    def summed(ref, count):
        total = ref[0].astype(F32)
        for i in range(1, count):
            total = total + ref[i].astype(F32)
        return total

    def unit_loop(fn):
        for i in range(1, QUAD):
            fn((unit + i) % QUAD)

    def z_loop(fn):
        lax.fori_loop(1, z_count, lambda i, c: (fn((z + i) % z_count), c)[1], 0)

    class Reduce:
        def __init__(self, ro, ri, zo, zi, go, gi, rss, rsr, zs, zr, gs, gr):
            self.refs = (ro, ri, zo, zi, go, gi)
            self.rs = lambda i: rc(ro.at[i], ri.at[unit], rss.at[i], rsr.at[unit], at_unit(i))
            self.rw = lambda i: rc(ro.at[i], ri.at[i], rss.at[i], rsr.at[i], at_unit(i))
            self.zs = lambda i: rc(zo, zi.at[z], zs.at[i], zr.at[z], at_z(i))
            self.zw = lambda i: rc(zo, zi.at[i], zs.at[i], zr.at[i], at_z(i))
            self.gs = lambda i: rc(go, gi.at[unit], gs.at[i], gr.at[unit], at_unit(i))
            self.gw = lambda i: rc(go, gi.at[i], gs.at[i], gr.at[i], at_unit(i))

        def scatter(self):
            ro, ri = self.refs[:2]
            unit_loop(lambda i: self.rs(i).start())
            ri[unit] = ro[unit]

        def across(self):
            ro, ri, zo, zi = self.refs[:4]
            unit_loop(lambda i: self.rw(i).wait_recv())
            zo[...] = summed(ri, QUAD).astype(BF16)
            z_loop(lambda i: self.zs(i).start())
            zi[z] = zo[...]

        def gather(self):
            zi, go, gi = self.refs[3:]
            z_loop(lambda i: self.zw(i).wait_recv())
            go[...] = summed(zi, z_count).astype(BF16)
            unit_loop(lambda i: self.gs(i).start())
            gi[unit] = go[...]

        def finish(self):
            unit_loop(lambda i: self.gw(i).wait_recv())

        def drain(self):
            unit_loop(lambda i: self.rw(i).wait_send())
            z_loop(lambda i: self.zw(i).wait_send())
            unit_loop(lambda i: self.gw(i).wait_send())

    first = Reduce(rs1_out, rs1_in, z1_out, z1_in, g1_out, g1_in, rs1_s, rs1_r, z1_s, z1_r, g1_s, g1_r)
    second = Reduce(rs2_out, rs2_in, z2_out, z2_in, g2_out, g2_in, rs2_s, rs2_r, z2_s, z2_r, g2_s, g2_r)

    head_loop(lambda i: rc(down_out, down_in.at[i], down_s.at[i], down_r.at[i], at_head(i)).wait_recv())
    down_act = summed(down_in, head_count).astype(BF16)
    up_query = (2.0 * dot(down_act[0:8, :], dq_ref[...])).astype(BF16)
    up_key = (2.0 * dot(down_act[8:16, :], key_grad)).astype(BF16)
    up_value = (2.0 * dot(down_act[16:24, :], value_grad)).astype(BF16)
    chunk = width // QUAD
    for i in range(QUAD):
        rs1_out[i, 0:8, :] = up_query[:, i * chunk : (i + 1) * chunk]
        rs1_out[i, 8:16, 0:HEAD_SIZE] = up_key
        rs1_out[i, 8:16, HEAD_SIZE:] = up_value
    first.scatter()
    first.across()

    head_loop(lambda i: rc(back_out, back_in.at[i], back_s.at[i], back_r.at[i], at_head(i)).wait_recv())
    back_act = summed(back_in, head_count).astype(BF16)
    down_grad = (2.0 * dot(back_act, x_ref[...])).astype(BF16)
    for i in range(QUAD):
        rs2_out[i] = down_grad[:, i * chunk : (i + 1) * chunk]
    second.scatter()
    second.across()
    first.gather()
    second.gather()
    first.finish()
    for i in range(QUAD):
        guq_ref[:, i * chunk : (i + 1) * chunk] = g1_in[i, 0:8, :].astype(F32)
    gukv_ref[0:8, :] = g1_out[8:16, 0:HEAD_SIZE].astype(F32)
    gukv_ref[8:16, :] = g1_out[8:16, HEAD_SIZE:].astype(F32)
    second.finish()
    for i in range(QUAD):
        gd_ref[:, i * chunk : (i + 1) * chunk] = g2_in[i].astype(F32)

    @pl.when(core == 0)
    def _():
        kv_copy(place + 1).wait_send()

    lax.fori_loop(chip + 1, QUAD, lambda i, c: (kv_copy(2 * i + core).wait_send(), c)[1], 0)

    def drain_block(i, carry):
        j = 2 * i + core
        rc(kv_all.at[j], kv_all.at[j], fw_s.at[j], kv_r.at[j], partner).wait_send()
        return carry

    lax.fori_loop(0, chip, drain_block, 0)
    lax.fori_loop(0, place, lambda j, c: (part_copy_pair(j).wait_send(), c)[1], 0)
    head_loop(lambda i: rc(down_out, down_in.at[i], down_s.at[i], down_r.at[i], at_head(i)).wait_send())
    head_loop(lambda i: rc(back_out, back_in.at[i], back_s.at[i], back_r.at[i], at_head(i)).wait_send())
    first.drain()
    second.drain()


def body(x, q, k, v, do, wd, uq, ukv):
    rows, width = q.shape
    seq_count = lax.axis_size("seq")
    head_count = lax.axis_size("head")
    heads = width // HEAD_SIZE
    features = x.shape[1]
    chunk = width // QUAD
    z_count = seq_count // QUAD
    vmem = pl.BlockSpec(memory_space=pltpu.VMEM)
    dma = pltpu.SemaphoreType.DMA
    reduce_bufs = []
    for depth in (16, 24):
        reduce_bufs += [
            pltpu.VMEM((QUAD, depth, chunk), BF16),
            pltpu.VMEM((QUAD, depth, chunk), BF16),
            pltpu.VMEM((depth, chunk), BF16),
            pltpu.VMEM((z_count, depth, chunk), BF16),
            pltpu.VMEM((depth, chunk), BF16),
            pltpu.VMEM((QUAD, depth, chunk), BF16),
        ]
    reduce_sems = [dma((n,)) for n in (QUAD, QUAD, z_count, z_count, QUAD, QUAD)] * 2
    outs = pl.pallas_call(
        functools.partial(kernel, seq_count, head_count),
        out_shape=(
            jax.ShapeDtypeStruct((rows, width), BF16),
            jax.ShapeDtypeStruct((rows, HEAD_SIZE), BF16),
            jax.ShapeDtypeStruct((rows, HEAD_SIZE), BF16),
            jax.ShapeDtypeStruct((24, features), F32),
            jax.ShapeDtypeStruct((8, width), F32),
            jax.ShapeDtypeStruct((16, HEAD_SIZE), F32),
        ),
        in_specs=[vmem] * 8,
        out_specs=(vmem,) * 6,
        scratch_shapes=[
            pltpu.VMEM((GROUP, 2, rows, HEAD_SIZE), BF16),
            pltpu.VMEM((GROUP, HEAD_SIZE, rows), BF16),
            pltpu.VMEM((heads * rows, HEAD_SIZE), BF16),
            pltpu.VMEM((heads * rows, HEAD_SIZE), BF16),
            pltpu.VMEM((GROUP, rows, heads * rows), F32),
            pltpu.VMEM((GROUP, rows, heads * rows), F32),
            pltpu.VMEM((GROUP, heads, 1, rows), F32),
            pltpu.VMEM((heads, 1, rows), F32),
            pltpu.VMEM((heads, 1, rows), F32),
            pltpu.VMEM((heads, 1, rows), F32),
            pltpu.VMEM((rows, heads * rows), BF16),
            pltpu.VMEM((rows, heads * rows), BF16),
            pltpu.VMEM((HEAD_SIZE, heads * rows), F32),
            pltpu.VMEM((2, rows, HEAD_SIZE), F32),
            pltpu.VMEM((GROUP, 2, rows, HEAD_SIZE), BF16),
            pltpu.VMEM((GROUP, 2, rows, HEAD_SIZE), BF16),
            pltpu.VMEM((QUAD, 2, rows, HEAD_SIZE), BF16),
            pltpu.VMEM((24, rows), BF16),
            pltpu.VMEM((head_count, 24, rows), BF16),
            pltpu.VMEM((24, rows), BF16),
            pltpu.VMEM((head_count, 24, rows), BF16),
        ]
        + reduce_bufs
        + [dma((GROUP,)), dma((GROUP,)), dma((GROUP,)), dma((GROUP,)), dma((GROUP,)), dma((QUAD,))]
        + [dma((head_count,))] * 4
        + reduce_sems,
        compiler_params=pltpu.CompilerParams(
            collective_id=0, has_side_effects=True, vmem_limit_bytes=60 * 1024 * 1024
        ),
    )(
        q,
        k,
        v,
        do,
        x,
        wd.reshape(24, features),
        uq,
        ukv.reshape(16, HEAD_SIZE),
    )
    dq, dk, dv, gd, guq, gukv = outs
    return (dq, dk, dv, gd.reshape(3, 8, features), guq, gukv.reshape(2, 8, HEAD_SIZE))


def solution(mesh):
    tokens = P("seq", "head")
    return jax.shard_map(
        body,
        mesh=mesh,
        in_specs=(tokens,) * 5 + (P(None, None, "head"), P(None, "head"), P(None, None, "head")),
        out_specs=(tokens,) * 3 + (P(None, None, "head"), P(None, "head"), P(None, None, "head")),
        check_vma=False,
    )
```

time: 417 us -> 62.5 us (0.15)
  waiting for transfers between devices: 238 us -> 0 us
  Pallas kernels: 0 us -> 55.8 us
  matrix products: 47.8 us -> 0 us
  starting transfers between devices: 38.1 us -> 0 us
  blocking collectives: 34.5 us -> 0 us
  other arithmetic: 25.6 us -> 0 us
  between operations: 14.4 us -> 0.66 us
  local copies, waits for them, and re-layouts: 17.4 us -> 5.74 us
    psum x1 -> x0, waiting for transfers between devices: 203 us -> none  [body(): lax.psum(down_local.astype(jnp.bfloat16), 'seq').astype(jnp.float32)]
    pallas_call x0 -> x1, Pallas kernels: none -> 55.8 us  [body(): pl.pallas_call(functools.partial(kernel, seq_count, head_count), out_shap...]
    dot_general x30 -> x0, matrix products: 47.8 us -> none  [the longest x4 14.7 us: head_block(): jnp.einsum('hqk,kd->qhd', prob_bf16, value_all, preferred_element_type=jn...]
    ppermute x14 -> x0, starting transfers between devices: 38.1 us -> none  [from_behind(): return lax.ppermute(value, axis, pairs)]
    psum x1 -> x0, blocking collectives: 34.5 us -> none  [body(): lax.psum(backward_piece.astype(jnp.bfloat16), 'head').astype(jnp.float32)]
    ppermute x14 -> x0, waiting for transfers between devices: 34.3 us -> none  [from_behind(): return lax.ppermute(value, axis, pairs)]
    reduce_sum x6 -> x0, other arithmetic: 10.3 us -> none  [the longest x4 4.9 us: head_block(): jnp.sum(jnp.exp(masked - row_top), axis=-1, keepdims=True)]
    dynamic_slice x8 -> x0, local copies, waits for them, and re-layouts: 4.8 us -> none  [body(): results = lax.map(head_block, (query_steps, grad_steps))]
  transfers between devices with their start and end apart: 15 -> 0, of which waited for: 13 -> 0; matrix products, arithmetic and copies ran while one was open for 4% -> 0% of each run, Pallas kernels for 0% -> 0%
where the time goes in v1:
time: 62.5 us; the launch traced here: 62.2 us
  Pallas kernels  55.8 us (89%)
  local copies, waits for them, and re-layouts  5.74 us (9%)
  between operations  0.66 us (1%)
    pallas_call x1, Pallas kernels, body(): pl.pallas_call(functools.partial(kernel, seq_count, head_count), out_shap...  55.8 us
    unnamed x16, local copies, waits for them, and re-layouts  5.74 us

profile of v1, /device:TPU:1, one launch (start us, length us, event | category | flops | bytes accessed | tf_op | source)
XLA Modules:
  0.0 62.2 jit_solution(9795710163413168477)
XLA Ops:
  0.6 55.8 %shard_map.127 = (bf16[256,1024]{1,0:T(8,128)(2,1)}, bf16[256,128]{1,0:T(8,128)(2,1)}, bf16[256,128]{1,0:T(8,128)(2,1)}, f32[24,1024]{1,0:T(8,128)}, f32[8,1024]{1,0:T(8,128)}, /*index=5*/f32[16,128]{1,0:T(8,128)}) custom-call(bf16[256,1024]{1,0:T(8,128)(2,1)} %q_ref.1, bf16[256,128]{1,0:T(8,128)(2,1)} %k_ref.1, bf16[256,128]{1,0:T(8,128)(2,1)} %v_ref.1, ...), custom_call_target="tpu_custom_call" | custom-call | tf_op jit(solution)/shard_map/pallas_call | solution.py:434
  56.4 0.0 copy-start.2
  56.4 1.9 %copy.20 = bf16[256,1024]{1,0:T(8,128)(2,1)} copy(bf16[256,1024]{1,0:T(8,128)(2,1)} %get-tuple-element.24) | data formatting | bytes 1048576
  58.3 0.0 copy-done.2
  58.3 0.0 copy-start.1
  58.3 0.6 %copy.21 = bf16[256,128]{1,0:T(8,128)(2,1)} copy(bf16[256,128]{1,0:T(8,128)(2,1)S(1)} %copy-done.2) | data formatting | bytes 131072
  58.9 0.2 copy-done.1
  59.2 0.0 copy-start
  59.2 0.6 %copy.22 = bf16[256,128]{1,0:T(8,128)(2,1)} copy(bf16[256,128]{1,0:T(8,128)(2,1)S(1)} %copy-done.1) | data formatting | bytes 131072
  59.8 0.3 copy-done
  60.1 0.0 copy-start.3
  60.1 0.6 %copy.23 = f32[3,8,1024]{2,1,0:T(8,128)} copy(f32[3,8,1024]{2,1,0:T(8,128)S(1)} %bitcast.4) | data formatting | bytes 196608
  60.7 0.1 copy-done.3
  60.8 0.0 copy-start.4
  60.8 0.6 copy.24
  61.5 0.1 copy-done.4
  61.6 0.6 copy.25
Async XLA Ops:
  56.4 1.9 %copy-start.2 = (bf16[256,128]{1,0:T(8,128)(2,1)S(1)}, bf16[256,128]{1,0:T(8,128)(2,1)}, u32[]{:S(2)}) copy-start(bf16[256,128]{1,0:T(8,128)(2,1)} %get-tuple-element.25) | copy-start | bytes 196612
  58.3 0.9 %copy-start.1 = (bf16[256,128]{1,0:T(8,128)(2,1)S(1)}, bf16[256,128]{1,0:T(8,128)(2,1)}, u32[]{:S(2)}) copy-start(bf16[256,128]{1,0:T(8,128)(2,1)} %get-tuple-element.26) | copy-start | bytes 196612
  59.2 0.9 %copy-start = (f32[24,1024]{1,0:T(8,128)S(1)}, f32[24,1024]{1,0:T(8,128)}, u32[]{:S(2)}) copy-start(f32[24,1024]{1,0:T(8,128)} %get-tuple-element.15) | copy-start | bytes 294916
  60.1 0.8 %copy-start.3 = (f32[8,1024]{1,0:T(8,128)S(1)}, f32[8,1024]{1,0:T(8,128)}, u32[]{:S(2)}) copy-start(f32[8,1024]{1,0:T(8,128)} %get-tuple-element.28) | copy-start | bytes 98308
  60.8 0.7 %copy-start.4 = (f32[16,128]{1,0:T(8,128)S(1)}, f32[16,128]{1,0:T(8,128)}, u32[]{:S(2)}) copy-start(f32[16,128]{1,0:T(8,128)} %get-tuple-element.17) | copy-start | bytes 24580

commit v2 on v1

--- a/solution.py
+++ b/solution.py
@@ -15,6 +15,7 @@
 BF16 = jnp.bfloat16
 GROUP = 8
 QUAD = 4
+WIDE = 2
 NT = (((1,), (1,)), ((), ()))
 
 
@@ -29,24 +30,32 @@
 def kernel(
     seq_count,
     head_count,
-    q_ref,
-    k_ref,
-    v_ref,
-    do_ref,
-    x_ref,
-    wd_ref,
-    uq_ref,
-    ukv_ref,
+    q_hbm,
+    k_hbm,
+    v_hbm,
+    do_hbm,
+    x_hbm,
+    wd_hbm,
+    uq_hbm,
+    ukv_hbm,
     dq_ref,
     dk_ref,
     dv_ref,
     gd_ref,
     guq_ref,
     gukv_ref,
+    q_ref,
+    k_ref,
+    do_ref,
+    x_ref,
+    wd_ref,
+    uq_ref,
+    ukv_ref,
     kv_all,
     kt_all,
     q_rot,
     do_hm,
+    dqt_b,
     e_buf,
     dp_buf,
     m_blk,
@@ -76,6 +85,9 @@
     z2_in,
     g2_out,
     g2_in,
+    z_hop,
+    x_hop,
+    in_s,
     kv_s,
     kv_r,
     fw_s,
@@ -134,39 +146,66 @@
 
     barrier = pltpu.get_barrier_semaphore()
 
-    def greet(i, carry):
-        pl.semaphore_signal(barrier, inc=1, device_id=at_place((place + i) % GROUP), device_id_type=MESH)
-        pl.semaphore_signal(barrier, inc=1, device_id=at_head((h + i) % head_count), device_id_type=MESH)
-        pl.semaphore_signal(barrier, inc=1, device_id=at_z((z + i) % z_count), device_id_type=MESH)
-        return carry
-
-    lax.fori_loop(1, 8, greet, 0)
+    def signal(sem, dev):
+        pl.semaphore_signal(sem, inc=1, device_id=dev, device_id_type=MESH)
+
+    x_count = head_count // 2
+    x_base = h - h % x_count
+    z_near = (at_z((z + 1) % z_count), at_z((z + z_count - 1) % z_count))
+    x_near = (
+        at_head(x_base + (h + 1) % x_count),
+        at_head(x_base + (h + x_count - 1) % x_count),
+    )
+
+    lax.fori_loop(1, GROUP, lambda i, c: (signal(barrier, at_place((place + i) % GROUP)), c)[1], 0)
+    for dev in z_near + x_near + (at_head((h + x_count) % head_count),):
+        signal(barrier, dev)
+
+    def z_tell(n):
+        for dev in z_near:
+            signal(z_hop.at[n], dev)
+
+    def x_tell(n):
+        for dev in x_near:
+            signal(x_hop.at[n], dev)
+
+    loads = [
+        pltpu.make_async_copy(src, dst, in_s.at[i])
+        for i, (src, dst) in enumerate(
+            (
+                (k_hbm, k_ref),
+                (v_hbm, kv_all.at[place, 1]),
+                (q_hbm, q_ref),
+                (do_hbm, do_ref),
+                (x_hbm, x_ref),
+                (wd_hbm, wd_ref),
+                (uq_hbm, uq_ref),
+                (ukv_hbm, ukv_ref),
+            )
+        )
+    ]
+    for load in loads:
+        load.start()
 
     half = HEAD_SIZE // 2
-    lane = lax.broadcasted_iota(jnp.int32, (1, HEAD_SIZE), 1)
-    feature = (lane % half).astype(F32)
+    feature = lax.broadcasted_iota(jnp.int32, (half, 1), 0).astype(F32)
     frequency = POSITION_SCALE * jnp.exp(feature * (-2.0 / HEAD_SIZE * 9.210340371976184))
-    position = (s * rows + lax.broadcasted_iota(jnp.int32, (rows, 1), 0)).astype(F32)
-    angle = position * frequency
+    position = (s * rows + lax.broadcasted_iota(jnp.int32, (1, rows), 1)).astype(F32)
+    angle = frequency * position
     cosine = jnp.cos(angle)
-    sine = jnp.where(lane < half, -1.0, 1.0) * jnp.sin(angle)
-
-    def rotate(x):
-        return x * cosine + pltpu.roll(x, half, 1) * sine
-
-    def unrotate(x):
-        return x * cosine - pltpu.roll(x, half, 1) * sine
-
-    kv_all[place, 0] = rotate(k_ref[...].astype(F32)).astype(BF16)
-    kv_all[place, 1] = v_ref[...]
-    down_out[...] = dot_nt(wd_ref[...], x_ref[...]).astype(BF16)
-    down_in[h] = down_out[...]
-    for i in range(heads):
-        cols = slice(i * HEAD_SIZE, (i + 1) * HEAD_SIZE)
-        q_rot[i * rows : (i + 1) * rows, :] = rotate(q_ref[:, cols].astype(F32)).astype(BF16)
-        do_hm[i * rows : (i + 1) * rows, :] = do_ref[:, cols]
-
-    pl.semaphore_wait(barrier, 21)
+    sine = jnp.sin(angle)
+
+    def turned(x, sn):
+        lo = x[:half, :]
+        hi = x[half:, :]
+        return jnp.concatenate([lo * cosine - hi * sn, hi * cosine + lo * sn], axis=0).astype(BF16)
+
+    loads[0].wait()
+    loads[1].wait()
+    own_t = turned(k_ref[...].T.astype(F32), sine)
+    kt_all[place] = own_t
+    kv_all[place, 0] = own_t.T
+    pl.semaphore_wait(barrier, 12)
 
     def kv_copy(q):
         return rc(kv_all.at[place], kv_all.at[place], kv_s.at[q], kv_r.at[place], at_place(q))
@@ -180,20 +219,34 @@
         return carry
 
     lax.fori_loop(chip + 1, QUAD, kv_start, 0)
+    z_tell(0)
+    x_tell(0)
+
+    loads[2].wait()
+    loads[3].wait()
+    for i in range(heads):
+        cols = slice(i * HEAD_SIZE, (i + 1) * HEAD_SIZE)
+        span = slice(i * rows, (i + 1) * rows)
+        q_rot[span, :] = turned(q_ref[:, cols].T.astype(F32), sine).T
+        do_hm[span, :] = do_ref[:, cols]
 
     def head_loop(fn):
         lax.fori_loop(1, head_count, lambda i, c: (fn((h + i) % head_count), c)[1], 0)
-
-    head_loop(lambda i: rc(down_out, down_in.at[h], down_s.at[i], down_r.at[h], at_head(i)).start())
 
     def forward_block(j, masked):
         keys = kv_all[j, 0]
         values = kv_all[j, 1]
-        kt_all[j] = keys.T
+        if not masked:
+            kt_all[j] = keys.T
         for i in range(heads):
             span = slice(i * rows, (i + 1) * rows)
-            st = dot_nt(keys, q_rot[span, :])
-            dp = dot_nt(values, do_hm[span, :])
+            if i % WIDE == 0:
+                part = slice(i * rows, (i + WIDE) * rows)
+                st_wide = dot_nt(keys, q_rot[part, :])
+                dp_wide = dot_nt(values, do_hm[part, :])
+            here = slice((i % WIDE) * rows, (i % WIDE + 1) * rows)
+            st = st_wide[:, here]
+            dp = dp_wide[:, here]
             if masked:
                 key_pos = lax.broadcasted_iota(jnp.int32, (rows, rows), 0)
                 query_pos = lax.broadcasted_iota(jnp.int32, (rows, rows), 1)
@@ -214,22 +267,56 @@
             e_buf[j, :, span] = e
             dp_buf[j, :, span] = dp
 
+    pl.semaphore_wait(x_hop.at[0], 2)
+    x_tell(1)
+    pl.semaphore_wait(z_hop.at[0], 2)
+    z_tell(1)
     forward_block(place, True)
-
-    def forward_step(u, carry):
-        par = u % 2
-        j = 2 * (chip - u // 2) + core + par * (1 - 2 * core)
+    pl.semaphore_wait(x_hop.at[1], 2)
+    pl.semaphore_wait(z_hop.at[1], 2)
+    z_tell(2)
+
+    for load in loads[4:]:
+        load.wait()
+    down_out[...] = dot_nt(wd_ref[...], x_ref[...]).astype(BF16)
+    down_in[h] = down_out[...]
+    head_loop(lambda i: rc(down_out, down_in.at[h], down_s.at[i], down_r.at[h], at_head(i)).start())
+
+    def kv_arrived(j):
         rc(kv_all.at[j], kv_all.at[j], kv_s.at[j], kv_r.at[j], partner).wait_recv()
 
-        @pl.when(par == 0)
+    def relay(j):
+        kv_arrived(j)
+        rc(kv_all.at[j], kv_all.at[j], fw_s.at[j], kv_r.at[j], partner).start()
+
+    @pl.when(core == 1)
+    def _():
+        kv_arrived(place - 1)
+        forward_block(place - 1, False)
+
+    @pl.when(chip > 0)
+    def _():
+        relay(place - 2)
+
+    def forward_step(n, carry):
+        i = n // 2
+        par = n % 2
+        base = 2 * (chip - 1 - i)
+
+        @pl.when(par == 1)
         def _():
-            rc(kv_all.at[j], kv_all.at[j], fw_s.at[j], kv_r.at[j], partner).start()
-
-        forward_block(j, False)
+            @pl.when(i < chip - 1)
+            def _():
+                relay(base - 2 + core)
+
+            kv_arrived(base + 1 - core)
+
+        forward_block(base + core + par * (1 - 2 * core), False)
         return carry
 
-    lax.fori_loop(2 - core, 2 * chip + 2, forward_step, 0)
-
+    lax.fori_loop(0, 2 * chip, forward_step, 0)
+
+    pl.semaphore_wait(z_hop.at[2], 2)
     for i in range(heads):
         inv = 1.0 / l_run[i]
         l_run[i] = inv
@@ -244,8 +331,14 @@
             prob = e_buf[j, :, span] * scale
             p_t[:, span] = prob.astype(BF16)
             ds_t[:, span] = (prob * (dp_buf[j, :, span] - d_run[i])).astype(BF16)
+            if i % 4 == 3:
+                part = slice((i - 3) * rows, (i + 1) * rows)
+                key_new = dot(ds_t[:, part], q_rot[part, :])
+                value_new = dot(p_t[:, part], do_hm[part, :])
+                key_part = key_new if i == 3 else key_part + key_new
+                value_part = value_new if i == 3 else value_part + value_new
         dq_t[...] += dot(kt_all[j], ds_t[...])
-        return dot(ds_t[...], q_rot[...]), dot(p_t[...], do_hm[...])
+        return key_part, value_part
 
     def part_copy_pair(j):
         return rc(part_out.at[j], pair_in.at[j], part_s.at[j], pair_r.at[j], partner)
@@ -278,14 +371,13 @@
     acc[0] = key_part
     acc[1] = value_part
 
-    back = jnp.zeros((8, rows), F32)
     for i in range(heads):
         span = slice(i * rows, (i + 1) * rows)
         cols = slice(i * HEAD_SIZE, (i + 1) * HEAD_SIZE)
-        grad = unrotate(dq_t[:, span].T * score_scale).astype(BF16)
-        dq_ref[:, cols] = grad
-        back += dot_nt(uq_ref[:, cols], grad)
-    back_out[0:8, :] = back.astype(BF16)
+        grad = turned(dq_t[:, span] * score_scale, -sine)
+        dqt_b[cols, :] = grad
+        dq_ref[:, cols] = grad.T
+    back_out[0:8, :] = dot(uq_ref[...], dqt_b[...]).astype(BF16)
 
     @pl.when(core == 0)
     def _():
@@ -298,12 +390,10 @@
         return carry
 
     lax.fori_loop(chip + 1, QUAD, chip_add, 0)
-    key_grad = unrotate(acc[0] * score_scale).astype(BF16)
-    value_grad = acc[1].astype(BF16)
-    dk_ref[...] = key_grad
-    dv_ref[...] = value_grad
-    back_out[8:16, :] = dot_nt(ukv_ref[0:8, :], key_grad).astype(BF16)
-    back_out[16:24, :] = dot_nt(ukv_ref[8:16, :], value_grad).astype(BF16)
+    key_grad = turned(acc[0].T * score_scale, -sine)
+    dv_ref[...] = acc[1].astype(BF16)
+    back_out[8:16, :] = dot(ukv_ref[0:8, :], key_grad).astype(BF16)
+    back_out[16:24, :] = dot_nt(ukv_ref[8:16, :], dv_ref[...]).astype(BF16)
     back_in[h] = back_out[...]
     head_loop(lambda i: rc(back_out, back_in.at[h], back_s.at[i], back_r.at[h], at_head(i)).start())
 
@@ -360,11 +450,13 @@
     first = Reduce(rs1_out, rs1_in, z1_out, z1_in, g1_out, g1_in, rs1_s, rs1_r, z1_s, z1_r, g1_s, g1_r)
     second = Reduce(rs2_out, rs2_in, z2_out, z2_in, g2_out, g2_in, rs2_s, rs2_r, z2_s, z2_r, g2_s, g2_r)
 
+    dk_ref[...] = key_grad.T
+
     head_loop(lambda i: rc(down_out, down_in.at[i], down_s.at[i], down_r.at[i], at_head(i)).wait_recv())
     down_act = summed(down_in, head_count).astype(BF16)
     up_query = (2.0 * dot(down_act[0:8, :], dq_ref[...])).astype(BF16)
-    up_key = (2.0 * dot(down_act[8:16, :], key_grad)).astype(BF16)
-    up_value = (2.0 * dot(down_act[16:24, :], value_grad)).astype(BF16)
+    up_key = (2.0 * dot(down_act[8:16, :], dk_ref[...])).astype(BF16)
+    up_value = (2.0 * dot(down_act[16:24, :], dv_ref[...])).astype(BF16)
     chunk = width // QUAD
     for i in range(QUAD):
         rs1_out[i, 0:8, :] = up_query[:, i * chunk : (i + 1) * chunk]
@@ -410,6 +502,14 @@
     second.drain()
 
 
+def hand_over(*refs):
+    copies = [pltpu.make_async_copy(refs[i], refs[6 + i], refs[12].at[i]) for i in range(6)]
+    for copy in copies:
+        copy.start()
+    for copy in copies:
+        copy.wait()
+
+
 def body(x, q, k, v, do, wd, uq, ukv):
     rows, width = q.shape
     seq_count = lax.axis_size("seq")
@@ -419,6 +519,7 @@
     chunk = width // QUAD
     z_count = seq_count // QUAD
     vmem = pl.BlockSpec(memory_space=pltpu.VMEM)
+    hbm = pl.BlockSpec(memory_space=pl.ANY)
     dma = pltpu.SemaphoreType.DMA
     reduce_bufs = []
     for depth in (16, 24):
@@ -434,20 +535,28 @@
     outs = pl.pallas_call(
         functools.partial(kernel, seq_count, head_count),
         out_shape=(
-            jax.ShapeDtypeStruct((rows, width), BF16),
-            jax.ShapeDtypeStruct((rows, HEAD_SIZE), BF16),
-            jax.ShapeDtypeStruct((rows, HEAD_SIZE), BF16),
-            jax.ShapeDtypeStruct((24, features), F32),
-            jax.ShapeDtypeStruct((8, width), F32),
-            jax.ShapeDtypeStruct((16, HEAD_SIZE), F32),
+            pltpu.VMEM((rows, width), BF16),
+            pltpu.VMEM((rows, HEAD_SIZE), BF16),
+            pltpu.VMEM((rows, HEAD_SIZE), BF16),
+            pltpu.VMEM((24, features), F32),
+            pltpu.VMEM((8, width), F32),
+            pltpu.VMEM((16, HEAD_SIZE), F32),
         ),
-        in_specs=[vmem] * 8,
+        in_specs=[hbm] * 8,
         out_specs=(vmem,) * 6,
         scratch_shapes=[
+            pltpu.VMEM((rows, width), BF16),
+            pltpu.VMEM((rows, HEAD_SIZE), BF16),
+            pltpu.VMEM((rows, width), BF16),
+            pltpu.VMEM((rows, features), BF16),
+            pltpu.VMEM((24, features), BF16),
+            pltpu.VMEM((8, width), BF16),
+            pltpu.VMEM((16, HEAD_SIZE), BF16),
             pltpu.VMEM((GROUP, 2, rows, HEAD_SIZE), BF16),
             pltpu.VMEM((GROUP, HEAD_SIZE, rows), BF16),
             pltpu.VMEM((heads * rows, HEAD_SIZE), BF16),
             pltpu.VMEM((heads * rows, HEAD_SIZE), BF16),
+            pltpu.VMEM((width, rows), BF16),
             pltpu.VMEM((GROUP, rows, heads * rows), F32),
             pltpu.VMEM((GROUP, rows, heads * rows), F32),
             pltpu.VMEM((GROUP, heads, 1, rows), F32),
@@ -467,11 +576,14 @@
             pltpu.VMEM((head_count, 24, rows), BF16),
         ]
         + reduce_bufs
-        + [dma((GROUP,)), dma((GROUP,)), dma((GROUP,)), dma((GROUP,)), dma((GROUP,)), dma((QUAD,))]
+        + [pltpu.SemaphoreType.REGULAR((3,)), pltpu.SemaphoreType.REGULAR((2,))]
+        + [dma((8,))]
+        + [dma((GROUP,))] * 5
+        + [dma((QUAD,))]
         + [dma((head_count,))] * 4
         + reduce_sems,
         compiler_params=pltpu.CompilerParams(
-            collective_id=0, has_side_effects=True, vmem_limit_bytes=60 * 1024 * 1024
+            collective_id=0, has_side_effects=True, vmem_limit_bytes=54 * 1024 * 1024
         ),
     )(
         q,
@@ -483,7 +595,13 @@
         uq,
         ukv.reshape(16, HEAD_SIZE),
     )
-    dq, dk, dv, gd, guq, gukv = outs
+    dq, dk, dv, gd, guq, gukv = pl.pallas_call(
+        hand_over,
+        out_shape=tuple(jax.ShapeDtypeStruct(o.shape, o.dtype) for o in outs),
+        in_specs=[vmem] * 6,
+        out_specs=(hbm,) * 6,
+        scratch_shapes=[dma((6,))],
+    )(*[pltpu.with_memory_space_constraint(o, pltpu.VMEM) for o in outs])
     return (dq, dk, dv, gd.reshape(3, 8, features), guq, gukv.reshape(2, 8, HEAD_SIZE))
 
 

time: 62.5 us -> 54.5 us (0.87)
  local copies, waits for them, and re-layouts: 5.74 us -> 0 us
  Pallas kernels: 55.8 us -> 53.8 us
    unnamed x16 -> x0, local copies, waits for them, and re-layouts: 5.74 us -> none
    pallas_call x1, Pallas kernels: 55.8 us -> 52.9 us  [body(): pl.pallas_call(functools.partial(kernel, seq_count, head_count), out_shap...]
    pallas_call x0 -> x1, Pallas kernels: none -> 0.92 us  [body(): pl.pallas_call(hand_over, out_shape=tuple((jax.ShapeDtypeStruct(o.shape,...]
where the time goes in v2:
time: 54.5 us; the launch traced here: 54.4 us
  Pallas kernels  53.8 us (99%)
  between operations  0.64 us (1%)
    pallas_call x1, Pallas kernels, body(): pl.pallas_call(functools.partial(kernel, seq_count, head_count), out_shap...  52.9 us

profile of v2, /device:TPU:1, one launch (start us, length us, event | category | flops | bytes accessed | tf_op | source)
XLA Modules:
  0.0 54.4 jit_solution(5508543254964215259)
XLA Ops:
  0.6 52.9 %shard_map.127 = (bf16[256,1024]{1,0:T(8,128)(2,1)S(1)}, bf16[256,128]{1,0:T(8,128)(2,1)S(1)}, bf16[256,128]{1,0:T(8,128)(2,1)S(1)}, f32[24,1024]{1,0:T(8,128)S(...) custom-call(bf16[256,1024]{1,0:T(8,128)(2,1)} %q_hbm.1, bf16[256,128]{1,0:T(8,128)(2,1)} %k_hbm.1, ...), custom_call_target="tpu_custom_call" | custom-call | tf_op jit(solution)/shard_map/pallas_call | solution.py:535
  53.5 0.9 %shard_map.128 = (bf16[256,1024]{1,0:T(8,128)(2,1)}, bf16[256,128]{1,0:T(8,128)(2,1)}, bf16[256,128]{1,0:T(8,128)(2,1)}, f32[24,1024]{1,0:T(8,128)}, f32[8,1024]{1,0:T(8,128)}, /*index=5*/f32[16,128]{1,0:T(8,128)}) custom-call(bf16[256,1024]{1,0:T(8,128)(2,1)S(1)} %get-tuple-element.18.refs_0_, bf16[256,128]{1,0:T(8,128)(2,1)S(1)} %get-tuple-element.19.refs_1_, ...), custom_call_target="tpu_custom_call" | custom-call | tf_op jit(solution)/shard_map/pallas_call | solution.py:598

commit v3 on v2

--- a/solution.py
+++ b/solution.py
@@ -69,6 +69,10 @@
     part_out,
     pair_in,
     chip_in,
+    table,
+    mini_out,
+    mini_in,
+    back_kv,
     down_out,
     down_in,
     back_out,
@@ -94,6 +98,8 @@
     part_s,
     pair_r,
     chip_r,
+    mini_s,
+    mini_r,
     down_s,
     down_r,
     back_s,
@@ -195,10 +201,13 @@
     cosine = jnp.cos(angle)
     sine = jnp.sin(angle)
 
-    def turned(x, sn):
+    def turned_by(x, cs, sn):
         lo = x[:half, :]
         hi = x[half:, :]
-        return jnp.concatenate([lo * cosine - hi * sn, hi * cosine + lo * sn], axis=0).astype(BF16)
+        return jnp.concatenate([lo * cs - hi * sn, hi * cs + lo * sn], axis=0).astype(BF16)
+
+    def turned(x, sn):
+        return turned_by(x, cosine, sn)
 
     loads[0].wait()
     loads[1].wait()
@@ -267,56 +276,66 @@
             e_buf[j, :, span] = e
             dp_buf[j, :, span] = dp
 
+    forward_block(place, True)
     pl.semaphore_wait(x_hop.at[0], 2)
     x_tell(1)
     pl.semaphore_wait(z_hop.at[0], 2)
     z_tell(1)
-    forward_block(place, True)
+
+    def table_step(i, carry):
+        away = (s + seq_count - place + 2 * i + core) % seq_count - s
+        turn = frequency * (away * rows).astype(F32)
+        cs = jnp.cos(turn)
+        sn = jnp.sin(turn)
+        table[i, 0] = cosine * cs - sine * sn
+        table[i, 1] = sine * cs + cosine * sn
+        return carry
+
+    lax.fori_loop(0, chip, table_step, 0)
+
+    def kv_arrived(j):
+        rc(kv_all.at[j], kv_all.at[j], kv_s.at[j], kv_r.at[j], partner).wait_recv()
+
+    def relay(j):
+        kv_arrived(j)
+        rc(kv_all.at[j], kv_all.at[j], fw_s.at[j], kv_r.at[j], partner).start()
+
+    @pl.when(core == 1)
+    def _():
+        kv_arrived(place - 1)
+        forward_block(place - 1, False)
+
+    @pl.when(chip > 0)
+    def _():
+        relay(place - 2)
+
+    def forward_step(n, carry):
+        i = n // 2
+        par = n % 2
+        base = 2 * (chip - 1 - i)
+
+        @pl.when(par == 1)
+        def _():
+            @pl.when(i < chip - 1)
+            def _():
+                relay(base - 2 + core)
+
+            kv_arrived(base + 1 - core)
+
+        forward_block(base + core + par * (1 - 2 * core), False)
+        return carry
+
+    lax.fori_loop(0, 2 * chip, forward_step, 0)
+
     pl.semaphore_wait(x_hop.at[1], 2)
     pl.semaphore_wait(z_hop.at[1], 2)
     z_tell(2)
-
     for load in loads[4:]:
         load.wait()
     down_out[...] = dot_nt(wd_ref[...], x_ref[...]).astype(BF16)
     down_in[h] = down_out[...]
     head_loop(lambda i: rc(down_out, down_in.at[h], down_s.at[i], down_r.at[h], at_head(i)).start())
 
-    def kv_arrived(j):
-        rc(kv_all.at[j], kv_all.at[j], kv_s.at[j], kv_r.at[j], partner).wait_recv()
-
-    def relay(j):
-        kv_arrived(j)
-        rc(kv_all.at[j], kv_all.at[j], fw_s.at[j], kv_r.at[j], partner).start()
-
-    @pl.when(core == 1)
-    def _():
-        kv_arrived(place - 1)
-        forward_block(place - 1, False)
-
-    @pl.when(chip > 0)
-    def _():
-        relay(place - 2)
-
-    def forward_step(n, carry):
-        i = n // 2
-        par = n % 2
-        base = 2 * (chip - 1 - i)
-
-        @pl.when(par == 1)
-        def _():
-            @pl.when(i < chip - 1)
-            def _():
-                relay(base - 2 + core)
-
-            kv_arrived(base + 1 - core)
-
-        forward_block(base + core + par * (1 - 2 * core), False)
-        return carry
-
-    lax.fori_loop(0, 2 * chip, forward_step, 0)
-
-    pl.semaphore_wait(z_hop.at[2], 2)
     for i in range(heads):
         inv = 1.0 / l_run[i]
         l_run[i] = inv
@@ -346,6 +365,15 @@
     def part_copy_chip(j):
         return rc(part_out.at[j], chip_in.at[chip], part_s.at[j], chip_r.at[chip], at_place(j))
 
+    def back_rows(key_sum, value_sum, cs, sn):
+        key_back = turned_by(key_sum.T * score_scale, cs, -sn)
+        return jnp.concatenate(
+            [dot(ukv_ref[0:8, :], key_back), dot_nt(ukv_ref[8:16, :], value_sum)], axis=0
+        )
+
+    def mini_copy(i):
+        return rc(mini_out.at[i], mini_in.at[chip], mini_s.at[i], mini_r.at[chip], at_place(2 * i + core))
+
     def backward_step(w, carry):
         par = w % 2
         j = 2 * (w // 2) + (1 - core) + par * (2 * core - 1)
@@ -360,8 +388,13 @@
         @pl.when(par == 1)
         def _():
             part_copy_pair(j).wait_recv()
-            part_out[j, 0] = (key_part + pair_in[j, 0].astype(F32)).astype(BF16)
-            part_out[j, 1] = (value_part + pair_in[j, 1].astype(F32)).astype(BF16)
+            key_sum = key_part + pair_in[j, 0].astype(F32)
+            value_sum = (value_part + pair_in[j, 1].astype(F32)).astype(BF16)
+            i = w // 2
+            mini_out[i] = back_rows(key_sum, value_sum, table[i, 0], table[i, 1]).astype(BF16)
+            mini_copy(i).start()
+            part_out[j, 0] = key_sum.astype(BF16)
+            part_out[j, 1] = value_sum
             part_copy_chip(j).start()
 
         return carry
@@ -370,6 +403,8 @@
     key_part, value_part = backward_block(place)
     acc[0] = key_part
     acc[1] = value_part
+
+    pl.semaphore_wait(z_hop.at[2], 2)
 
     for i in range(heads):
         span = slice(i * rows, (i + 1) * rows)
@@ -384,18 +419,26 @@
         rc(part_out.at[place], pair_in.at[place], part_s.at[place], pair_r.at[place], partner).wait_recv()
         acc[...] += pair_in[place].astype(F32)
 
+    back_kv[...] = back_rows(acc[0], acc[1].astype(BF16), cosine, sine)
+
+    def mini_add(i, carry):
+        rc(mini_out.at[0], mini_in.at[i], mini_s.at[0], mini_r.at[i], at_place(2 * i + core)).wait_recv()
+        back_kv[...] += mini_in[i].astype(F32)
+        return carry
+
+    lax.fori_loop(chip + 1, QUAD, mini_add, 0)
+    back_out[8:24, :] = back_kv[...].astype(BF16)
+    back_in[h] = back_out[...]
+    head_loop(lambda i: rc(back_out, back_in.at[h], back_s.at[i], back_r.at[h], at_head(i)).start())
+
     def chip_add(i, carry):
         rc(part_out.at[place], chip_in.at[i], part_s.at[place], chip_r.at[i], at_place(2 * i + core)).wait_recv()
         acc[...] += chip_in[i].astype(F32)
         return carry
 
     lax.fori_loop(chip + 1, QUAD, chip_add, 0)
-    key_grad = turned(acc[0].T * score_scale, -sine)
+    dk_ref[...] = turned(acc[0].T * score_scale, -sine).T
     dv_ref[...] = acc[1].astype(BF16)
-    back_out[8:16, :] = dot(ukv_ref[0:8, :], key_grad).astype(BF16)
-    back_out[16:24, :] = dot_nt(ukv_ref[8:16, :], dv_ref[...]).astype(BF16)
-    back_in[h] = back_out[...]
-    head_loop(lambda i: rc(back_out, back_in.at[h], back_s.at[i], back_r.at[h], at_head(i)).start())
 
     def summed(ref, count):
         total = ref[0].astype(F32)
@@ -450,7 +493,6 @@
     first = Reduce(rs1_out, rs1_in, z1_out, z1_in, g1_out, g1_in, rs1_s, rs1_r, z1_s, z1_r, g1_s, g1_r)
     second = Reduce(rs2_out, rs2_in, z2_out, z2_in, g2_out, g2_in, rs2_s, rs2_r, z2_s, z2_r, g2_s, g2_r)
 
-    dk_ref[...] = key_grad.T
 
     head_loop(lambda i: rc(down_out, down_in.at[i], down_s.at[i], down_r.at[i], at_head(i)).wait_recv())
     down_act = summed(down_in, head_count).astype(BF16)
@@ -495,6 +537,7 @@
         return carry
 
     lax.fori_loop(0, chip, drain_block, 0)
+    lax.fori_loop(0, chip, lambda i, c: (mini_copy(i).wait_send(), c)[1], 0)
     lax.fori_loop(0, place, lambda j, c: (part_copy_pair(j).wait_send(), c)[1], 0)
     head_loop(lambda i: rc(down_out, down_in.at[i], down_s.at[i], down_r.at[i], at_head(i)).wait_send())
     head_loop(lambda i: rc(back_out, back_in.at[i], back_s.at[i], back_r.at[i], at_head(i)).wait_send())
@@ -570,6 +613,10 @@
             pltpu.VMEM((GROUP, 2, rows, HEAD_SIZE), BF16),
             pltpu.VMEM((GROUP, 2, rows, HEAD_SIZE), BF16),
             pltpu.VMEM((QUAD, 2, rows, HEAD_SIZE), BF16),
+            pltpu.VMEM((QUAD, 2, HEAD_SIZE // 2, rows), F32),
+            pltpu.VMEM((QUAD, 16, rows), BF16),
+            pltpu.VMEM((QUAD, 16, rows), BF16),
+            pltpu.VMEM((16, rows), F32),
             pltpu.VMEM((24, rows), BF16),
             pltpu.VMEM((head_count, 24, rows), BF16),
             pltpu.VMEM((24, rows), BF16),
@@ -579,7 +626,7 @@
         + [pltpu.SemaphoreType.REGULAR((3,)), pltpu.SemaphoreType.REGULAR((2,))]
         + [dma((8,))]
         + [dma((GROUP,))] * 5
-        + [dma((QUAD,))]
+        + [dma((QUAD,))] * 3
         + [dma((head_count,))] * 4
         + reduce_sems,
         compiler_params=pltpu.CompilerParams(

time: 54.5 us -> 52.1 us (0.956)
  Pallas kernels: 53.8 us -> 51.4 us
    pallas_call x1, Pallas kernels: 52.9 us -> 50.4 us  [body(): pl.pallas_call(functools.partial(kernel, seq_count, head_count), out_shap...]
where the time goes in v3:
time: 52.1 us; the launch traced here: 52 us
  Pallas kernels  51.4 us (99%)
  between operations  0.64 us (1%)
    pallas_call x1, Pallas kernels, body(): pl.pallas_call(functools.partial(kernel, seq_count, head_count), out_shap...  50.4 us

profile of v3, /device:TPU:1, one launch (start us, length us, event | category | flops | bytes accessed | tf_op | source)
XLA Modules:
  0.0 52.0 jit_solution(7054646062639296183)
XLA Ops:
  0.6 50.4 %shard_map.127 = (bf16[256,1024]{1,0:T(8,128)(2,1)S(1)}, bf16[256,128]{1,0:T(8,128)(2,1)S(1)}, bf16[256,128]{1,0:T(8,128)(2,1)S(1)}, f32[24,1024]{1,0:T(8,128)S(...) custom-call(bf16[256,1024]{1,0:T(8,128)(2,1)} %q_hbm.1, bf16[256,128]{1,0:T(8,128)(2,1)} %k_hbm.1, ...), custom_call_target="tpu_custom_call" | custom-call | tf_op jit(solution)/shard_map/pallas_call | solution.py:578
  51.1 0.9 %shard_map.128 = (bf16[256,1024]{1,0:T(8,128)(2,1)}, bf16[256,128]{1,0:T(8,128)(2,1)}, bf16[256,128]{1,0:T(8,128)(2,1)}, f32[24,1024]{1,0:T(8,128)}, f32[8,1024]{1,0:T(8,128)}, /*index=5*/f32[16,128]{1,0:T(8,128)}) custom-call(bf16[256,1024]{1,0:T(8,128)(2,1)S(1)} %get-tuple-element.18.refs_0_, bf16[256,128]{1,0:T(8,128)(2,1)S(1)} %get-tuple-element.19.refs_1_, ...), custom_call_target="tpu_custom_call" | custom-call | tf_op jit(solution)/shard_map/pallas_call | solution.py:645

commit v4 on v3

--- a/solution.py
+++ b/solution.py
@@ -282,28 +282,26 @@
     pl.semaphore_wait(z_hop.at[0], 2)
     z_tell(1)
 
-    def table_step(i, carry):
-        away = (s + seq_count - place + 2 * i + core) % seq_count - s
+    def kv_arrived(j):
+        rc(kv_all.at[j], kv_all.at[j], kv_s.at[j], kv_r.at[j], partner).wait_recv()
+
+    def relay(j):
+        kv_arrived(j)
+        rc(kv_all.at[j], kv_all.at[j], fw_s.at[j], kv_r.at[j], partner).start()
+
+    @pl.when(core == 1)
+    def _():
+        kv_arrived(place - 1)
+        forward_block(place - 1, False)
+
+    @pl.when(chip > 0)
+    def _():
+        away = (s + seq_count - 2) % seq_count - s
         turn = frequency * (away * rows).astype(F32)
         cs = jnp.cos(turn)
         sn = jnp.sin(turn)
-        table[i, 0] = cosine * cs - sine * sn
-        table[i, 1] = sine * cs + cosine * sn
-        return carry
-
-    lax.fori_loop(0, chip, table_step, 0)
-
-    def kv_arrived(j):
-        rc(kv_all.at[j], kv_all.at[j], kv_s.at[j], kv_r.at[j], partner).wait_recv()
-
-    def relay(j):
-        kv_arrived(j)
-        rc(kv_all.at[j], kv_all.at[j], fw_s.at[j], kv_r.at[j], partner).start()
-
-    @pl.when(core == 1)
-    def _():
-        kv_arrived(place - 1)
-        forward_block(place - 1, False)
+        table[0] = cosine * cs - sine * sn
+        table[1] = sine * cs + cosine * sn
 
     @pl.when(chip > 0)
     def _():
@@ -371,8 +369,8 @@
             [dot(ukv_ref[0:8, :], key_back), dot_nt(ukv_ref[8:16, :], value_sum)], axis=0
         )
 
-    def mini_copy(i):
-        return rc(mini_out.at[i], mini_in.at[chip], mini_s.at[i], mini_r.at[chip], at_place(2 * i + core))
+    def mini_copy(q):
+        return rc(mini_out, mini_in, mini_s.at[0], mini_r.at[0], at_place(q))
 
     def backward_step(w, carry):
         par = w % 2
@@ -390,9 +388,12 @@
             part_copy_pair(j).wait_recv()
             key_sum = key_part + pair_in[j, 0].astype(F32)
             value_sum = (value_part + pair_in[j, 1].astype(F32)).astype(BF16)
-            i = w // 2
-            mini_out[i] = back_rows(key_sum, value_sum, table[i, 0], table[i, 1]).astype(BF16)
-            mini_copy(i).start()
+
+            @pl.when(w // 2 == chip - 1)
+            def _():
+                mini_out[...] = back_rows(key_sum, value_sum, table[0], table[1]).astype(BF16)
+                mini_copy(place - 2).start()
+
             part_out[j, 0] = key_sum.astype(BF16)
             part_out[j, 1] = value_sum
             part_copy_chip(j).start()
@@ -419,24 +420,27 @@
         rc(part_out.at[place], pair_in.at[place], part_s.at[place], pair_r.at[place], partner).wait_recv()
         acc[...] += pair_in[place].astype(F32)
 
-    back_kv[...] = back_rows(acc[0], acc[1].astype(BF16), cosine, sine)
-
-    def mini_add(i, carry):
-        rc(mini_out.at[0], mini_in.at[i], mini_s.at[0], mini_r.at[i], at_place(2 * i + core)).wait_recv()
-        back_kv[...] += mini_in[i].astype(F32)
-        return carry
-
-    lax.fori_loop(chip + 1, QUAD, mini_add, 0)
-    back_out[8:24, :] = back_kv[...].astype(BF16)
-    back_in[h] = back_out[...]
-    head_loop(lambda i: rc(back_out, back_in.at[h], back_s.at[i], back_r.at[h], at_head(i)).start())
-
     def chip_add(i, carry):
         rc(part_out.at[place], chip_in.at[i], part_s.at[place], chip_r.at[i], at_place(2 * i + core)).wait_recv()
         acc[...] += chip_in[i].astype(F32)
         return carry
 
-    lax.fori_loop(chip + 1, QUAD, chip_add, 0)
+    lax.fori_loop(chip + 2, QUAD, chip_add, 0)
+    back_kv[...] = back_rows(acc[0], acc[1].astype(BF16), cosine, sine)
+
+    @pl.when(chip < QUAD - 1)
+    def _():
+        mini_copy(place + 2).wait_recv()
+        back_kv[...] += mini_in[...].astype(F32)
+
+    back_out[8:24, :] = back_kv[...].astype(BF16)
+    back_in[h] = back_out[...]
+    head_loop(lambda i: rc(back_out, back_in.at[h], back_s.at[i], back_r.at[h], at_head(i)).start())
+
+    @pl.when(chip < QUAD - 1)
+    def _():
+        chip_add(chip + 1, 0)
+
     dk_ref[...] = turned(acc[0].T * score_scale, -sine).T
     dv_ref[...] = acc[1].astype(BF16)
 
@@ -505,7 +509,6 @@
         rs1_out[i, 8:16, 0:HEAD_SIZE] = up_key
         rs1_out[i, 8:16, HEAD_SIZE:] = up_value
     first.scatter()
-    first.across()
 
     head_loop(lambda i: rc(back_out, back_in.at[i], back_s.at[i], back_r.at[i], at_head(i)).wait_recv())
     back_act = summed(back_in, head_count).astype(BF16)
@@ -513,6 +516,7 @@
     for i in range(QUAD):
         rs2_out[i] = down_grad[:, i * chunk : (i + 1) * chunk]
     second.scatter()
+    first.across()
     second.across()
     first.gather()
     second.gather()
@@ -537,7 +541,11 @@
         return carry
 
     lax.fori_loop(0, chip, drain_block, 0)
-    lax.fori_loop(0, chip, lambda i, c: (mini_copy(i).wait_send(), c)[1], 0)
+
+    @pl.when(chip > 0)
+    def _():
+        mini_copy(place - 2).wait_send()
+
     lax.fori_loop(0, place, lambda j, c: (part_copy_pair(j).wait_send(), c)[1], 0)
     head_loop(lambda i: rc(down_out, down_in.at[i], down_s.at[i], down_r.at[i], at_head(i)).wait_send())
     head_loop(lambda i: rc(back_out, back_in.at[i], back_s.at[i], back_r.at[i], at_head(i)).wait_send())
@@ -613,9 +621,9 @@
             pltpu.VMEM((GROUP, 2, rows, HEAD_SIZE), BF16),
             pltpu.VMEM((GROUP, 2, rows, HEAD_SIZE), BF16),
             pltpu.VMEM((QUAD, 2, rows, HEAD_SIZE), BF16),
-            pltpu.VMEM((QUAD, 2, HEAD_SIZE // 2, rows), F32),
-            pltpu.VMEM((QUAD, 16, rows), BF16),
-            pltpu.VMEM((QUAD, 16, rows), BF16),
+            pltpu.VMEM((2, HEAD_SIZE // 2, rows), F32),
+            pltpu.VMEM((16, rows), BF16),
+            pltpu.VMEM((16, rows), BF16),
             pltpu.VMEM((16, rows), F32),
             pltpu.VMEM((24, rows), BF16),
             pltpu.VMEM((head_count, 24, rows), BF16),
@@ -626,7 +634,7 @@
         + [pltpu.SemaphoreType.REGULAR((3,)), pltpu.SemaphoreType.REGULAR((2,))]
         + [dma((8,))]
         + [dma((GROUP,))] * 5
-        + [dma((QUAD,))] * 3
+        + [dma((QUAD,)), dma((1,)), dma((1,))]
         + [dma((head_count,))] * 4
         + reduce_sems,
         compiler_params=pltpu.CompilerParams(

time: 52.1 us -> 52.2 us (level)
  no operation moved by 1% of the time
where the time goes in v4:
time: 52.2 us; the launch traced here: 52.1 us
  Pallas kernels  51.4 us (98%)
  between operations  0.64 us (1%)
    pallas_call x1, Pallas kernels, body(): pl.pallas_call(functools.partial(kernel, seq_count, head_count), out_shap...  50.5 us

profile of v4, /device:TPU:1, one launch (start us, length us, event | category | flops | bytes accessed | tf_op | source)
XLA Modules:
  0.0 52.1 jit_solution(13365052702592291785)
XLA Ops:
  0.6 50.5 %shard_map.127 = (bf16[256,1024]{1,0:T(8,128)(2,1)S(1)}, bf16[256,128]{1,0:T(8,128)(2,1)S(1)}, bf16[256,128]{1,0:T(8,128)(2,1)S(1)}, f32[24,1024]{1,0:T(8,128)S(...) custom-call(bf16[256,1024]{1,0:T(8,128)(2,1)} %q_hbm.1, bf16[256,128]{1,0:T(8,128)(2,1)} %k_hbm.1, ...), custom_call_target="tpu_custom_call" | custom-call | tf_op jit(solution)/shard_map/pallas_call | solution.py:586
  51.2 0.9 %shard_map.128 = (bf16[256,1024]{1,0:T(8,128)(2,1)}, bf16[256,128]{1,0:T(8,128)(2,1)}, bf16[256,128]{1,0:T(8,128)(2,1)}, f32[24,1024]{1,0:T(8,128)}, f32[8,1024]{1,0:T(8,128)}, /*index=5*/f32[16,128]{1,0:T(8,128)}) custom-call(bf16[256,1024]{1,0:T(8,128)(2,1)S(1)} %get-tuple-element.18.refs_0_, bf16[256,128]{1,0:T(8,128)(2,1)S(1)} %get-tuple-element.19.refs_1_, ...), custom_call_target="tpu_custom_call" | custom-call | tf_op jit(solution)/shard_map/pallas_call | solution.py:653
